TPU v7x, 32 devices: a whole 2x2x4 slice. The times are simulated.
32 devices in a mesh: outer: 4 (over z), inner: 2 (over x), head: 4 (over y, core).
Axes of the slice: x: 2, y: 2, z: 4, core: 2. Of those that a mesh axis runs over, the one named last changes fastest.
Arguments:
- queries: bfloat16 [8192, 1024], P(('outer', 'inner'), 'head'), may hold values from -10 to 10
- keys: bfloat16 [8192, 128], P(('outer', 'inner', 'head')), may hold values from -10 to 10
- values: bfloat16 [8192, 128], P(('outer', 'inner', 'head')), may hold values from -6 to 6
- doc_lengths: int32 [4], replicated, may hold values from 1 to 3584, as said below
- block_count: int32 [8], replicated, may hold values from 1 to 2, as said below
Outputs:
- attended: bfloat16 [8192, 1024], P(('outer', 'inner'), 'head')
Inputs may be any that keep to these rules, and one draw needn't show every extreme that they name: `doc_lengths`: the lengths sum to 6144, and one rollout has exactly 3584 tokens. `block_count`: exactly half of the 8 context devices hold 2 blocks and the others 1; where 8 >= 16, 8 consecutive context devices hold 1 block each; the blocks follow one another in device order.
All inputs are finite; a program needn't handle non-finite values.
Results may differ from a plain program's by a relative error of at most 0.0032.
Values may be sent and summed in bfloat16 or wider, within the bound.
No kernel may reach another device: no remote copies, remote signals or barrier semaphores. Data moves between devices by JAX's collectives and lax.ppermute only.
A program may use at most 64 MiB of HBM per device.

v0:
```python
import functools
import math

import jax
import jax.numpy as jnp
from jax import lax
from jax.experimental import pallas as pl
from jax.experimental.pallas import tpu as pltpu
from jax.sharding import PartitionSpec as P

BLOCK = 512
REACH = 7
PAIR = 2
FIELDS = 6
NEGATIVE = -1e30
AXES = ("outer", "inner", "head")


def join_kernel(keys, values, joined, semaphores):
    rows = keys.shape[0]
    copies = [
        pltpu.make_async_copy(keys, joined.at[:rows], semaphores.at[0]),
        pltpu.make_async_copy(values, joined.at[rows:], semaphores.at[1]),
    ]
    for copy in copies:
        copy.start()
    for copy in copies:
        copy.wait()


def join(keys, values):
    rows, dim = keys.shape
    return pl.pallas_call(
        join_kernel,
        out_shape=jax.ShapeDtypeStruct((2 * rows, dim), keys.dtype),
        in_specs=[pl.BlockSpec(memory_space=pl.ANY)] * 2,
        out_specs=pl.BlockSpec(memory_space=pltpu.VMEM),
        scratch_shapes=[pltpu.SemaphoreType.DMA((2,))],
        compiler_params=pltpu.CompilerParams(vmem_limit_bytes=4 << 20),
        name="join",
    )(keys, values)


def attend_kernel(cfg, place, lengths, counts, q_ref, *refs):
    delta, tiles, heads, tile_q, first, last, further = cfg
    piece_refs = refs[: PAIR * tiles]
    refs = refs[PAIR * tiles :]
    if last:
        top_all, acc_all, out_ref = refs[:3]
        refs = refs[3:]
    elif first:
        top_all, acc_all, flag = refs[:3]
        refs = refs[3:]
    else:
        top_all, acc_all = refs[2:4]
        refs = refs[4:]
    k_all, v_all, score_a, score_b, top, acc, starts, work = refs
    rows = q_ref.shape[0]
    dim = k_all.shape[2]
    tile_k = k_all.shape[1]
    piece = tile_k // PAIR
    spread = tiles // PAIR
    context = counts.shape[0]
    documents = lengths.shape[0]
    device = place[0]
    head_index = place[1]
    core = lax.rem(head_index, PAIR)
    side = head_index // PAIR
    scale = math.log2(math.e) / math.sqrt(dim)

    def fill(index, total):
        starts[index] = total
        return total + counts[index] * BLOCK

    starts[context] = lax.fori_loop(0, context, fill, jnp.int32(0))
    own_start = starts[device]
    own_live = counts[device] * BLOCK

    def opening(position):
        def look(index, carry):
            edge, begin = carry
            edge = edge + lengths[index]
            return edge, jnp.where(edge <= position, edge, begin)

        return lax.fori_loop(0, documents, look, (jnp.int32(0), jnp.int32(0)))[1]

    if first:
        def reaches(level, found):
            before = starts[(level - further + 1) * PAIR]
            return found | (opening(starts[level * PAIR]) < before).astype(jnp.int32)

        flag[0] = lax.fori_loop(further, context // PAIR, reaches, jnp.int32(0))

    for tile in range(tiles):
        for step in range(PAIR):
            source = piece_refs[tile * PAIR + step]
            slot = core if step == 0 else 1 - core
            at = pl.ds(pl.multiple_of(slot * piece, piece), piece)
            k_all[tile, at, :] = source[:piece, :]
            v_all[tile, at, :dim] = source[piece:, :]
        v_all[tile, :, dim:] = jnp.ones((tile_k, dim), jnp.bfloat16)

    def finish(index, acc_ref):
        at = pl.ds(pl.multiple_of(index * tile_q, tile_q), tile_q)
        for head in range(heads):
            out_ref[at, head * dim : (head + 1) * dim] = (
                acc_ref[head, :, :dim] / acc_ref[head, :, dim:]
            ).astype(jnp.bfloat16)

    def plan_queries(index, count):
        row = index * tile_q
        query_start = own_start + row
        query_end = query_start + tile_q - 1
        opened_low = opening(query_start)
        opened_high = opening(query_end)

        def plan_keys(tile, carry):
            count, opener = carry
            level = device // PAIR - delta
            member = lax.rem(device, PAIR)
            member = jnp.where(tile // spread == 1, 1 - member, member)
            source = jnp.maximum(level * PAIR + member, 0)
            offset = lax.rem(side + spread - lax.rem(tile, spread), spread) * tile_k
            key_start = starts[source] + offset
            key_end = key_start + tile_k - 1
            active = (
                (level >= 0)
                & (row < own_live)
                & (offset < counts[source] * BLOCK)
                & (key_start <= query_end)
                & (key_end >= opened_low)
            )
            whole = (key_end <= query_start) & (key_start >= opened_high)
            at = count * FIELDS
            work[at] = index
            work[at + 1] = tile
            work[at + 2] = whole.astype(jnp.int32)
            work[at + 3] = key_start
            work[at + 4] = opener
            work[at + 5] = 0
            return jnp.where(active, count + 1, count), jnp.where(active, 0, opener)

        after = lax.fori_loop(0, tiles, plan_keys, (count, jnp.int32(1)))[0]

        @pl.when(after > count)
        def _():
            work[(after - 1) * FIELDS + 5] = 1

        if last:

            @pl.when((after == count) & (row < own_live))
            def _():
                finish(index, acc_all.at[index])

            @pl.when(row >= own_live)
            def _():
                at = pl.ds(pl.multiple_of(row, tile_q), tile_q)
                out_ref[at, :] = jnp.zeros((tile_q, heads * dim), jnp.bfloat16)

        return after

    total = lax.fori_loop(0, rows // tile_q, plan_queries, jnp.int32(0))
    work[total * FIELDS] = 0
    work[total * FIELDS + 1] = 0

    def wide(value, times):
        return jnp.concatenate([value] * times, axis=1)

    def score(item, head):
        at = pl.ds(pl.multiple_of(work[item * FIELDS] * tile_q, tile_q), tile_q)
        return lax.dot_general(
            q_ref[at, head * dim : (head + 1) * dim],
            k_all[work[item * FIELDS + 1]],
            (((1,), (1,)), ((), ())),
            preferred_element_type=jnp.float32,
        )

    def handle(item, current, coming):
        base = item * FIELDS
        query_index = work[base]
        whole = work[base + 2]

        @pl.when(work[base + 4] == 1)
        def _():
            if first:
                top[...] = jnp.full(top.shape, NEGATIVE, jnp.float32)
                acc[...] = jnp.zeros(acc.shape, jnp.float32)
            else:
                top[...] = top_all[query_index]
                acc[...] = acc_all[query_index]

        def run(masked):
            v_tile = v_all[work[base + 1]]
            if masked:
                row = own_start + query_index * tile_q
                narrow = row + lax.broadcasted_iota(jnp.int32, (tile_q, dim), 0)

                def look(index, carry):
                    edge, begin = carry
                    edge = edge + lengths[index]
                    return edge, jnp.where(narrow >= edge, edge, begin)

                opened = lax.fori_loop(
                    0, documents, look, (jnp.int32(0), jnp.zeros((tile_q, dim), jnp.int32))
                )[1]
                key_position = work[base + 3] + lax.broadcasted_iota(
                    jnp.int32, (tile_q, tile_k), 1
                )
                visible = (key_position <= wide(narrow, tile_k // dim)) & (
                    key_position >= wide(opened, tile_k // dim)
                )
            for head in range(heads):
                coming[head] = score(item + 1, head)
                scores = current[head]
                if masked:
                    scores = jnp.where(visible, scores, NEGATIVE)
                before = top[head]
                after = jnp.maximum(before, jnp.max(scores, axis=1, keepdims=True))
                weights = jnp.exp2((scores - wide(after, tile_k // dim)) * scale)
                factor = jnp.exp2((before - after) * scale)
                top[head] = after
                acc[head] = acc[head] * wide(factor, 2) + jnp.dot(
                    weights.astype(jnp.bfloat16), v_tile, preferred_element_type=jnp.float32
                )

        @pl.when(whole == 1)
        def _():
            run(False)

        @pl.when(whole == 0)
        def _():
            run(True)

        @pl.when(work[base + 5] == 1)
        def _():
            if last:
                finish(query_index, acc)
            else:
                top_all[query_index] = top[...]
                acc_all[query_index] = acc[...]

    @pl.when(total > 0)
    def _():
        for head in range(heads):
            score_a[head] = score(0, head)

    def two(index, unused):
        handle(2 * index, score_a, score_b)

        @pl.when(2 * index + 1 < total)
        def _():
            handle(2 * index + 1, score_b, score_a)

        return 0

    lax.fori_loop(0, (total + 1) // 2, two, 0)


def attend(delta, place, lengths, counts, queries, pieces, state, last, further=0):
    rows, width = queries.shape
    piece_rows, dim = pieces[0].shape
    heads = width // dim
    tile_k = piece_rows // 2 * PAIR
    tiles = len(pieces) // PAIR
    tile_q = min(rows, BLOCK)
    steps = rows // tile_q
    first = state is None
    scalar = pl.BlockSpec(memory_space=pltpu.SMEM)
    vector = pl.BlockSpec(memory_space=pltpu.VMEM)
    top = (heads, tile_q, dim)
    acc = (heads, tile_q, 2 * dim)
    scratch = [
        pltpu.VMEM((tiles, tile_k, dim), jnp.bfloat16),
        pltpu.VMEM((tiles, tile_k, 2 * dim), jnp.bfloat16),
        pltpu.VMEM((heads, tile_q, tile_k), jnp.float32),
        pltpu.VMEM((heads, tile_q, tile_k), jnp.float32),
        pltpu.VMEM(top, jnp.float32),
        pltpu.VMEM(acc, jnp.float32),
        pltpu.SMEM((counts.shape[0] + 1,), jnp.int32),
        pltpu.SMEM((FIELDS * (steps * tiles + 2),), jnp.int32),
    ]
    aliases = {}
    if last:
        out_shape = jax.ShapeDtypeStruct((rows, width), jnp.bfloat16)
        out_specs = vector
    else:
        out_shape = (
            jax.ShapeDtypeStruct((steps,) + top, jnp.float32),
            jax.ShapeDtypeStruct((steps,) + acc, jnp.float32),
        )
        out_specs = (vector, vector)
        if first:
            out_shape += (jax.ShapeDtypeStruct((1,), jnp.int32),)
            out_specs += (scalar,)
        else:
            aliases = {4 + len(pieces): 0, 5 + len(pieces): 1}
    carried = () if first else state
    pairs = steps * tiles * heads
    return pl.pallas_call(
        functools.partial(attend_kernel, (delta, tiles, heads, tile_q, first, last, further)),
        out_shape=out_shape,
        in_specs=[scalar] * 3 + [vector] * (1 + len(pieces) + len(carried)),
        out_specs=out_specs,
        scratch_shapes=scratch,
        input_output_aliases=aliases,
        compiler_params=pltpu.CompilerParams(vmem_limit_bytes=24 << 20),
        cost_estimate=pl.CostEstimate(
            flops=pairs * tile_q * tile_k * dim * 4,
            bytes_accessed=pairs * tile_q * dim * 4,
            transcendentals=pairs * tile_q * tile_k,
        ),
    )(place, lengths, counts, queries, *pieces, *carried)


def solution(mesh):
    contexts = mesh.shape["outer"] * mesh.shape["inner"]
    group = mesh.shape["head"]
    levels = contexts // PAIR
    sides = group // PAIR
    farthest = min((REACH + PAIR - 1) // PAIR, levels - 1)
    near_count = min(farthest, 2)

    def moved(value, target):
        pairs = []
        for level in range(levels):
            for member in range(PAIR):
                for side in range(sides):
                    for core in range(PAIR):
                        place = (level, member, side, core)
                        to = target(*place)
                        pairs.append(tuple(
                            ((a * PAIR + b) * sides + c) * PAIR + d for a, b, c, d in (place, to)
                        ))
        return lax.ppermute(value, AXES, pairs)

    def ahead(value, delta):
        return moved(value, lambda l, m, s, c: ((l + delta) % levels, m, s, c))

    def spread(value):
        found = []
        for across in range(PAIR):
            for along in range(sides):
                held = value
                if across or along:
                    held = moved(
                        value, lambda l, m, s, c: (l, (m + across) % PAIR, (s + along) % sides, c)
                    )
                found += [held, moved(held, lambda l, m, s, c: (l, m, s, 1 - c))]
        return found

    def layer(queries, keys, values, lengths, counts):
        device = lax.axis_index(("outer", "inner"))
        place = jnp.stack([device, lax.axis_index("head")]).astype(jnp.int32)

        def step(delta, **rest):
            return attend(
                delta, place=place, lengths=lengths, counts=counts, queries=queries, **rest
            )

        own = join(keys, values)
        near = [own] + [ahead(own, delta) for delta in range(1, near_count + 1)]
        state = None
        reach = None
        for delta in range(near_count):
            state = step(
                delta,
                pieces=spread(near[delta]),
                state=state,
                last=False,
                further=near_count + 1,
            )
            if delta == 0:
                reach = state[2]
                state = state[:2]
        delta = near_count
        pieces = spread(near[delta])
        if farthest == delta:
            return step(delta, pieces=pieces, state=state, last=True)

        def short(operands):
            _, pieces, state = operands
            return step(delta, pieces=pieces, state=state, last=True)

        def long(operands):
            near, pieces, state = operands
            state = step(delta, pieces=pieces, state=state, last=False)
            for further in range(delta + 1, farthest + 1):
                near = ahead(near, 1)
                state = step(further, pieces=spread(near), state=state, last=further == farthest)
            return state

        return lax.cond(reach[0] != 0, long, short, (near[delta], pieces, state))

    placed = (
        P(("outer", "inner"), "head"),
        P(AXES, None),
        P(AXES, None),
        P(),
        P(),
    )
    return jax.shard_map(
        layer, mesh=mesh, in_specs=placed, out_specs=P(("outer", "inner"), "head"), check_vma=False
    )
```

profile of v0, /device:TPU:11, one launch (start us, length us, event | category | flops | bytes accessed | tf_op | source)
XLA Modules:
  0.0 49.4 jit_solution(17841174132229955619)
XLA Ops:
  0.0 0.8 %copy-done = bf16[256,128]{1,0:T(8,128)(2,1)S(1)} copy-done((bf16[256,128]{1,0:T(8,128)(2,1)S(1)}, bf16[256,128]{1,0:T(8,128)(2,1)}, u32[]{:S(2)}) %copy-start) | copy-done | bytes 65560
  0.8 0.8 %copy-done.1 = bf16[256,128]{1,0:T(8,128)(2,1)S(1)} copy-done((bf16[256,128]{1,0:T(8,128)(2,1)S(1)}, bf16[256,128]{1,0:T(8,128)(2,1)}, u32[]{:S(2)}) %copy-start.1) | copy-done | bytes 65560
  1.7 0.2 join.1.refs_0_
  1.8 1.3 %collective-permute-start.9 = (bf16[512,128]{1,0:T(8,128)(2,1)S(1)}, bf16[512,128]{1,0:T(8,128)(2,1)S(1)}, u32[]{:S(2)}, u32[]{:S(2)}) collective-permute-start(bf16[512,128]{1,0:T(8,128)(2,1)S(1)} %join.1.refs_0_), channel_id=1, source_target_pairs={{0,2},{1,3},{2,0},{3,1},{4,6},{5,7},{6,4},{7,5},{8,10},{9,11},{10,... | collective-permute-start | bytes 393224 | tf_op jit(solution)/shard_map/ppermute | solution.py:334
  3.1 0.3 collective-permute-start.11
  3.4 1.2 %collective-permute-start.13 = (bf16[512,128]{1,0:T(8,128)(2,1)S(1)}, bf16[512,128]{1,0:T(8,128)(2,1)S(1)}, u32[]{:S(2)}, u32[]{:S(2)}) collective-permute-start(bf16[512,128]{1,0:T(8,128)(2,1)S(1)} %join.1.refs_0_), channel_id=1, source_target_pairs={{0,6},{1,7},{2,4},{3,5},{4,2},{5,3},{6,0},{7,1},{8,14},{9,15},{10,... | collective-permute-start | bytes 393224 | tf_op jit(solution)/shard_map/ppermute | solution.py:334
  4.6 1.5 %collective-permute-start.8 = (bf16[512,128]{1,0:T(8,128)(2,1)S(1)}, bf16[512,128]{1,0:T(8,128)(2,1)S(1)}, u32[]{:S(2)}, u32[]{:S(2)}) collective-permute-start(bf16[512,128]{1,0:T(8,128)(2,1)S(1)} %join.1.refs_0_), channel_id=1, source_target_pairs={{0,1},{1,0},{2,3},{3,2},{4,5},{5,4},{6,7},{7,6},{8,9},{9,8},{10,11... | collective-permute-start | bytes 393224 | tf_op jit(solution)/shard_map/ppermute | solution.py:334
  6.1 1.3 %collective-permute-start.23 = (bf16[512,128]{1,0:T(8,128)(2,1)S(1)}, bf16[512,128]{1,0:T(8,128)(2,1)S(1)}, u32[]{:S(2)}, u32[]{:S(2)}) collective-permute-start(bf16[512,128]{1,0:T(8,128)(2,1)S(1)} %join.1.refs_0_), channel_id=1, source_target_pairs={{0,8},{1,9},{2,10},{3,11},{4,12},{5,13},{6,14},{7,15},{8,16},{9,17... | collective-permute-start | bytes 393224 | tf_op jit(solution)/shard_map/ppermute | solution.py:334
  7.4 1.2 %collective-permute-start.15 = (bf16[512,128]{1,0:T(8,128)(2,1)S(1)}, bf16[512,128]{1,0:T(8,128)(2,1)S(1)}, u32[]{:S(2)}, u32[]{:S(2)}) collective-permute-start(bf16[512,128]{1,0:T(8,128)(2,1)S(1)} %join.1.refs_0_), channel_id=1, source_target_pairs={{0,16},{1,17},{2,18},{3,19},{4,20},{5,21},{6,22},{7,23},{8,24},{9,... | collective-permute-start | bytes 393224 | tf_op jit(solution)/shard_map/ppermute | solution.py:334
  8.6 0.0 collective-permute-done.11.refs_4_
  8.6 2.0 %collective-permute-start.10 = (bf16[512,128]{1,0:T(8,128)(2,1)S(1)}, bf16[512,128]{1,0:T(8,128)(2,1)S(1)}, u32[]{:S(2)}, u32[]{:S(2)}) collective-permute-start(bf16[512,128]{1,0:T(8,128)(2,1)S(1)} %collective-permute-done.9.refs_2_), channel_id=1, source_target_pairs={{0,1},{1,0},{2,3},{3,2},{4,5},{5,4},{6,7},{7,6},{8,9},{9,8},{10,11... | collective-permute-start | bytes 393224 | tf_op jit(solution)/shard_map/ppermute | solution.py:334
  10.6 0.0 collective-permute-done.13.refs_6_
  10.6 1.2 %collective-permute-start.12 = (bf16[512,128]{1,0:T(8,128)(2,1)S(1)}, bf16[512,128]{1,0:T(8,128)(2,1)S(1)}, u32[]{:S(2)}, u32[]{:S(2)}) collective-permute-start(bf16[512,128]{1,0:T(8,128)(2,1)S(1)} %collective-permute-done.11.refs_4_), channel_id=1, source_target_pairs={{0,1},{1,0},{2,3},{3,2},{4,5},{5,4},{6,7},{7,6},{8,9},{9,8},{10,11... | collective-permute-start | bytes 393224 | tf_op jit(solution)/shard_map/ppermute | solution.py:334
  11.8 0.0 collective-permute-done.8.refs_1_
  11.8 0.0 collective-permute-start.14
  11.8 0.0 collective-permute-done.23.refs_0_
  11.8 1.3 %collective-permute-start.25 = (bf16[512,128]{1,0:T(8,128)(2,1)S(1)}, bf16[512,128]{1,0:T(8,128)(2,1)S(1)}, u32[]{:S(2)}, u32[]{:S(2)}) collective-permute-start(bf16[512,128]{1,0:T(8,128)(2,1)S(1)} %collective-permute-done.23.refs_0_), channel_id=1, source_target_pairs={{0,2},{1,3},{2,0},{3,1},{4,6},{5,7},{6,4},{7,5},{8,10},{9,11},{10,... | collective-permute-start | bytes 393224 | tf_op jit(solution)/shard_map/ppermute | solution.py:334
  13.1 2.7 %collective-permute-done.15 = bf16[512,128]{1,0:T(8,128)(2,1)S(1)} collective-permute-done((bf16[512,128]{1,0:T(8,128)(2,1)S(1)}, bf16[512,128]{1,0:T(8,128)(2,1)S(1)}, u32[]{:S(2)}, u32[]{:S(2)}) %collective-permute-start.15) | collective-permute-done | bytes 131104 | tf_op jit(solution)/shard_map/ppermute | solution.py:334
  15.8 0.3 collective-permute-start.27
  16.1 0.0 collective-permute-done.10.refs_3_
  16.1 2.2 %collective-permute-start.29 = (bf16[512,128]{1,0:T(8,128)(2,1)S(1)}, bf16[512,128]{1,0:T(8,128)(2,1)S(1)}, u32[]{:S(2)}, u32[]{:S(2)}) collective-permute-start(bf16[512,128]{1,0:T(8,128)(2,1)S(1)} %collective-permute-done.23.refs_0_), channel_id=1, source_target_pairs={{0,6},{1,7},{2,4},{3,5},{4,2},{5,3},{6,0},{7,1},{8,14},{9,15},{10,... | collective-permute-start | bytes 393224 | tf_op jit(solution)/shard_map/ppermute | solution.py:334
  18.3 0.0 collective-permute-done.12.refs_5_
  18.3 1.4 %collective-permute-start.24 = (bf16[512,128]{1,0:T(8,128)(2,1)S(1)}, bf16[512,128]{1,0:T(8,128)(2,1)S(1)}, u32[]{:S(2)}, u32[]{:S(2)}) collective-permute-start(bf16[512,128]{1,0:T(8,128)(2,1)S(1)} %collective-permute-done.23.refs_0_), channel_id=1, source_target_pairs={{0,1},{1,0},{2,3},{3,2},{4,5},{5,4},{6,7},{7,6},{8,9},{9,8},{10,11... | collective-permute-start | bytes 393224 | tf_op jit(solution)/shard_map/ppermute | solution.py:334
  19.7 0.2 collective-permute-start.17
  19.9 0.1 pad_add_fusion.place
  20.0 0.0 collective-permute-done.25.refs_2_
  20.0 0.3 collective-permute-start.19
  20.3 0.0 collective-permute-done.27.refs_4_
  20.3 2.2 %collective-permute-start.21 = (bf16[512,128]{1,0:T(8,128)(2,1)S(1)}, bf16[512,128]{1,0:T(8,128)(2,1)S(1)}, u32[]{:S(2)}, u32[]{:S(2)}) collective-permute-start(bf16[512,128]{1,0:T(8,128)(2,1)S(1)} %collective-permute-done.15), channel_id=1, source_target_pairs={{0,6},{1,7},{2,4},{3,5},{4,2},{5,3},{6,0},{7,1},{8,14},{9,15},{10,... | collective-permute-start | bytes 393224 | tf_op jit(solution)/shard_map/ppermute | solution.py:334
  22.5 1.3 %collective-permute-done.29.refs_6_ = bf16[512,128]{1,0:T(8,128)(2,1)S(1)} collective-permute-done((bf16[512,128]{1,0:T(8,128)(2,1)S(1)}, bf16[512,128]{1,0:T(8,128)(2,1)S(1)}, u32[]{:S(2)}, u32[]{:S(2)}) %collective-permute-start.29) | collective-permute-done | bytes 131104 | tf_op jit(solution)/shard_map/ppermute | solution.py:334
  23.8 3.0 %collective-permute-start.26 = (bf16[512,128]{1,0:T(8,128)(2,1)S(1)}, bf16[512,128]{1,0:T(8,128)(2,1)S(1)}, u32[]{:S(2)}, u32[]{:S(2)}) collective-permute-start(bf16[512,128]{1,0:T(8,128)(2,1)S(1)} %collective-permute-done.25.refs_2_), channel_id=1, source_target_pairs={{0,1},{1,0},{2,3},{3,2},{4,5},{5,4},{6,7},{7,6},{8,9},{9,8},{10,11... | collective-permute-start | bytes 393224 | tf_op jit(solution)/shard_map/ppermute | solution.py:334
  26.8 0.0 collective-permute-done.24.refs_1_
  26.8 0.0 collective-permute-start.28
  26.8 0.6 %collective-permute-done.17 = bf16[512,128]{1,0:T(8,128)(2,1)S(1)} collective-permute-done((bf16[512,128]{1,0:T(8,128)(2,1)S(1)}, bf16[512,128]{1,0:T(8,128)(2,1)S(1)}, u32[]{:S(2)}, u32[]{:S(2)}) %collective-permute-start.17) | collective-permute-done | bytes 131104 | tf_op jit(solution)/shard_map/ppermute | solution.py:334
  27.5 0.9 %collective-permute-start.30 = (bf16[512,128]{1,0:T(8,128)(2,1)S(1)}, bf16[512,128]{1,0:T(8,128)(2,1)S(1)}, u32[]{:S(2)}, u32[]{:S(2)}) collective-permute-start(bf16[512,128]{1,0:T(8,128)(2,1)S(1)} %collective-permute-done.29.refs_6_), channel_id=1, source_target_pairs={{0,1},{1,0},{2,3},{3,2},{4,5},{5,4},{6,7},{7,6},{8,9},{9,8},{10,11... | collective-permute-start | bytes 393224 | tf_op jit(solution)/shard_map/ppermute | solution.py:334
  28.4 7.6 %shard_map.57 = (f32[2,2,512,128]{3,2,1,0:T(8,128)S(1)}, f32[2,2,512,256]{3,2,1,0:T(8,128)S(1)}, s32[1]{0:T(128)}) custom-call(s32[2]{0:T(128)S(1)} %pad_add_fusion.place, s32[4]{0:T(128)} %lengths.3, s32[8]{0:T(128)} %counts.3, bf16[1024,256]{1,0:T(8,128)(2,1)} %q_ref.3, bf16[512,128]{1,0:T(8,128)(2,1)S(1)} %join.1.refs_0_, ...), custom_call_target="tpu_custom_call" | custom-call | flops 2147483648 | bytes 4194304 | tf_op jit(solution)/shard_map/pallas_call | solution.py:299
  36.7 0.0 collective-permute-done.19
  36.7 0.1 collective-permute-start.16
  36.8 0.0 collective-permute-done.21
  36.8 0.5 collective-permute-start.18
  37.3 0.1 collective-permute-start.20
  37.4 0.0 collective-permute-done.28.refs_5_
  37.4 0.4 collective-permute-start.22
  37.8 9.0 %shard_map.58 = (f32[2,2,512,128]{3,2,1,0:T(8,128)S(1)}, f32[2,2,512,256]{3,2,1,0:T(8,128)S(1)}) custom-call(s32[2]{0:T(128)S(1)} %pad_add_fusion.place, s32[4]{0:T(128)S(1)} %copy-done.3, s32[8]{0:T(128)S(1)} %copy-done.4, bf16[1024,256]{1,0:T(8,128)(2,1)S(1)} %copy-done.2, ...), custom_call_target="tpu_custom_call", output_to_operand_aliasing={{0}: (12, {}), {1}: (13, {})} | custom-call | flops 2147483648 | bytes 4194304 | tf_op jit(solution)/shard_map/pallas_call | solution.py:299
  46.9 1.7 %conditional.1 = (bf16[1024,256]{1,0:T(8,128)(2,1)S(1)}) conditional(s32[]{:T(128)} %bitcast.2, (s32[2]{0:T(128)S(1)}, s32[4]{0:T(128)S(1)}, s32[8]{0:T(128)S(1)}, bf16[1024,256]{1,0:T(8,128)(2,1)S(1)}, bf16[512,128]{1,0:T(8,128)(2,1)S(1)}, /*index=5*/bf16[512,128]{1,0:T(8,128)(2,1)S(1)}, bf16[512,128]{1,0:T(8,128)(2,1)S(1)}, ...), branch_computations={%region_0.0_spmd, %region_1.0_spmd} | conditional | flops 4294967296 | bytes 12583240 | solution.py:392
  46.9 1.5 %branch_0_fun.1 = bf16[1024,256]{1,0:T(8,128)(2,1)S(1)} custom-call(s32[2]{0:T(128)S(1)} %get-tuple-element.64.place, s32[4]{0:T(128)S(1)} %get-tuple-element.65.lengths, s32[8]{0:T(128)S(1)} %get-tuple-element.66.counts, bf16[1024,256]{1,0:T(8,128)(2,1)S(1)} %get-tuple-element.67.q_ref, bf16[512,128]{1,0:T(8,128)(2,1)S(1)} %get-tuple-element.68.refs_0_, ...), custom_call_target="tpu_custom_call" | custom-call | flops 2147483648 | bytes 4194304 | tf_op jit(solution)/shard_map/cond/branch_0_fun/pallas_call | solution.py:299
  48.6 0.0 copy-start.5
  48.6 0.8 %copy-done.5 = bf16[1024,256]{1,0:T(8,128)(2,1)} copy-done((bf16[1024,256]{1,0:T(8,128)(2,1)}, bf16[1024,256]{1,0:T(8,128)(2,1)S(1)}, u32[]{:S(2)}) %copy-start.5) | copy-done | bytes 524312
  (16 shorter events, 0.0 us)
Async XLA Ops:
  0.0 0.8 %copy-start = (bf16[256,128]{1,0:T(8,128)(2,1)S(1)}, bf16[256,128]{1,0:T(8,128)(2,1)}, u32[]{:S(2)}) copy-start(bf16[256,128]{1,0:T(8,128)(2,1)} %keys.1) | copy-start | bytes 196612
  0.8 0.8 %copy-start.1 = (bf16[256,128]{1,0:T(8,128)(2,1)S(1)}, bf16[256,128]{1,0:T(8,128)(2,1)}, u32[]{:S(2)}) copy-start(bf16[256,128]{1,0:T(8,128)(2,1)} %values.1) | copy-start | bytes 196612
  1.8 5.5 %collective-permute-start.9 = (bf16[512,128]{1,0:T(8,128)(2,1)S(1)}, bf16[512,128]{1,0:T(8,128)(2,1)S(1)}, u32[]{:S(2)}, u32[]{:S(2)}) collective-permute-start(bf16[512,128]{1,0:T(8,128)(2,1)S(1)} %join.1.refs_0_), channel_id=1, source_target_pairs={{0,2},{1,3},{2,0},{3,1},{4,6},{5,7},{6,4},{7,5},{8,10},{9,11},{10,... | collective-permute-start | bytes 393224 | tf_op jit(solution)/shard_map/ppermute | solution.py:334
  3.1 5.5 %collective-permute-start.11 = (bf16[512,128]{1,0:T(8,128)(2,1)S(1)}, bf16[512,128]{1,0:T(8,128)(2,1)S(1)}, u32[]{:S(2)}, u32[]{:S(2)}) collective-permute-start(bf16[512,128]{1,0:T(8,128)(2,1)S(1)} %join.1.refs_0_), channel_id=1, source_target_pairs={{0,4},{1,5},{2,6},{3,7},{4,0},{5,1},{6,2},{7,3},{8,12},{9,13},{10,... | collective-permute-start | bytes 393224 | tf_op jit(solution)/shard_map/ppermute | solution.py:334
  3.4 7.2 %collective-permute-start.13 = (bf16[512,128]{1,0:T(8,128)(2,1)S(1)}, bf16[512,128]{1,0:T(8,128)(2,1)S(1)}, u32[]{:S(2)}, u32[]{:S(2)}) collective-permute-start(bf16[512,128]{1,0:T(8,128)(2,1)S(1)} %join.1.refs_0_), channel_id=1, source_target_pairs={{0,6},{1,7},{2,4},{3,5},{4,2},{5,3},{6,0},{7,1},{8,14},{9,15},{10,... | collective-permute-start | bytes 393224 | tf_op jit(solution)/shard_map/ppermute | solution.py:334
  4.6 7.3 %collective-permute-start.8 = (bf16[512,128]{1,0:T(8,128)(2,1)S(1)}, bf16[512,128]{1,0:T(8,128)(2,1)S(1)}, u32[]{:S(2)}, u32[]{:S(2)}) collective-permute-start(bf16[512,128]{1,0:T(8,128)(2,1)S(1)} %join.1.refs_0_), channel_id=1, source_target_pairs={{0,1},{1,0},{2,3},{3,2},{4,5},{5,4},{6,7},{7,6},{8,9},{9,8},{10,11... | collective-permute-start | bytes 393224 | tf_op jit(solution)/shard_map/ppermute | solution.py:334
  6.1 5.8 %collective-permute-start.23 = (bf16[512,128]{1,0:T(8,128)(2,1)S(1)}, bf16[512,128]{1,0:T(8,128)(2,1)S(1)}, u32[]{:S(2)}, u32[]{:S(2)}) collective-permute-start(bf16[512,128]{1,0:T(8,128)(2,1)S(1)} %join.1.refs_0_), channel_id=1, source_target_pairs={{0,8},{1,9},{2,10},{3,11},{4,12},{5,13},{6,14},{7,15},{8,16},{9,17... | collective-permute-start | bytes 393224 | tf_op jit(solution)/shard_map/ppermute | solution.py:334
  7.4 8.5 %collective-permute-start.15 = (bf16[512,128]{1,0:T(8,128)(2,1)S(1)}, bf16[512,128]{1,0:T(8,128)(2,1)S(1)}, u32[]{:S(2)}, u32[]{:S(2)}) collective-permute-start(bf16[512,128]{1,0:T(8,128)(2,1)S(1)} %join.1.refs_0_), channel_id=1, source_target_pairs={{0,16},{1,17},{2,18},{3,19},{4,20},{5,21},{6,22},{7,23},{8,24},{9,... | collective-permute-start | bytes 393224 | tf_op jit(solution)/shard_map/ppermute | solution.py:334
  8.6 7.5 %collective-permute-start.10 = (bf16[512,128]{1,0:T(8,128)(2,1)S(1)}, bf16[512,128]{1,0:T(8,128)(2,1)S(1)}, u32[]{:S(2)}, u32[]{:S(2)}) collective-permute-start(bf16[512,128]{1,0:T(8,128)(2,1)S(1)} %collective-permute-done.9.refs_2_), channel_id=1, source_target_pairs={{0,1},{1,0},{2,3},{3,2},{4,5},{5,4},{6,7},{7,6},{8,9},{9,8},{10,11... | collective-permute-start | bytes 393224 | tf_op jit(solution)/shard_map/ppermute | solution.py:334
  10.6 7.6 %collective-permute-start.12 = (bf16[512,128]{1,0:T(8,128)(2,1)S(1)}, bf16[512,128]{1,0:T(8,128)(2,1)S(1)}, u32[]{:S(2)}, u32[]{:S(2)}) collective-permute-start(bf16[512,128]{1,0:T(8,128)(2,1)S(1)} %collective-permute-done.11.refs_4_), channel_id=1, source_target_pairs={{0,1},{1,0},{2,3},{3,2},{4,5},{5,4},{6,7},{7,6},{8,9},{9,8},{10,11... | collective-permute-start | bytes 393224 | tf_op jit(solution)/shard_map/ppermute | solution.py:334
  11.8 7.9 %collective-permute-start.14 = (bf16[512,128]{1,0:T(8,128)(2,1)S(1)}, bf16[512,128]{1,0:T(8,128)(2,1)S(1)}, u32[]{:S(2)}, u32[]{:S(2)}) collective-permute-start(bf16[512,128]{1,0:T(8,128)(2,1)S(1)} %collective-permute-done.13.refs_6_), channel_id=1, source_target_pairs={{0,1},{1,0},{2,3},{3,2},{4,5},{5,4},{6,7},{7,6},{8,9},{9,8},{10,11... | collective-permute-start | bytes 393224 | tf_op jit(solution)/shard_map/ppermute | solution.py:334
  11.8 8.2 %collective-permute-start.25 = (bf16[512,128]{1,0:T(8,128)(2,1)S(1)}, bf16[512,128]{1,0:T(8,128)(2,1)S(1)}, u32[]{:S(2)}, u32[]{:S(2)}) collective-permute-start(bf16[512,128]{1,0:T(8,128)(2,1)S(1)} %collective-permute-done.23.refs_0_), channel_id=1, source_target_pairs={{0,2},{1,3},{2,0},{3,1},{4,6},{5,7},{6,4},{7,5},{8,10},{9,11},{10,... | collective-permute-start | bytes 393224 | tf_op jit(solution)/shard_map/ppermute | solution.py:334
  15.8 4.5 %collective-permute-start.27 = (bf16[512,128]{1,0:T(8,128)(2,1)S(1)}, bf16[512,128]{1,0:T(8,128)(2,1)S(1)}, u32[]{:S(2)}, u32[]{:S(2)}) collective-permute-start(bf16[512,128]{1,0:T(8,128)(2,1)S(1)} %collective-permute-done.23.refs_0_), channel_id=1, source_target_pairs={{0,4},{1,5},{2,6},{3,7},{4,0},{5,1},{6,2},{7,3},{8,12},{9,13},{10,... | collective-permute-start | bytes 393224 | tf_op jit(solution)/shard_map/ppermute | solution.py:334
  16.1 7.7 %collective-permute-start.29 = (bf16[512,128]{1,0:T(8,128)(2,1)S(1)}, bf16[512,128]{1,0:T(8,128)(2,1)S(1)}, u32[]{:S(2)}, u32[]{:S(2)}) collective-permute-start(bf16[512,128]{1,0:T(8,128)(2,1)S(1)} %collective-permute-done.23.refs_0_), channel_id=1, source_target_pairs={{0,6},{1,7},{2,4},{3,5},{4,2},{5,3},{6,0},{7,1},{8,14},{9,15},{10,... | collective-permute-start | bytes 393224 | tf_op jit(solution)/shard_map/ppermute | solution.py:334
  18.3 8.6 %collective-permute-start.24 = (bf16[512,128]{1,0:T(8,128)(2,1)S(1)}, bf16[512,128]{1,0:T(8,128)(2,1)S(1)}, u32[]{:S(2)}, u32[]{:S(2)}) collective-permute-start(bf16[512,128]{1,0:T(8,128)(2,1)S(1)} %collective-permute-done.23.refs_0_), channel_id=1, source_target_pairs={{0,1},{1,0},{2,3},{3,2},{4,5},{5,4},{6,7},{7,6},{8,9},{9,8},{10,11... | collective-permute-start | bytes 393224 | tf_op jit(solution)/shard_map/ppermute | solution.py:334
  19.7 7.8 %collective-permute-start.17 = (bf16[512,128]{1,0:T(8,128)(2,1)S(1)}, bf16[512,128]{1,0:T(8,128)(2,1)S(1)}, u32[]{:S(2)}, u32[]{:S(2)}) collective-permute-start(bf16[512,128]{1,0:T(8,128)(2,1)S(1)} %collective-permute-done.15), channel_id=1, source_target_pairs={{0,2},{1,3},{2,0},{3,1},{4,6},{5,7},{6,4},{7,5},{8,10},{9,11},{10,... | collective-permute-start | bytes 393224 | tf_op jit(solution)/shard_map/ppermute | solution.py:334
  20.0 17.8 %copy-start.2 = (bf16[1024,256]{1,0:T(8,128)(2,1)S(1)}, bf16[1024,256]{1,0:T(8,128)(2,1)}, u32[]{:S(2)}) copy-start(bf16[1024,256]{1,0:T(8,128)(2,1)} %q_ref.3) | copy-start | bytes 1572868
  20.0 17.8 %copy-start.3 = (s32[4]{0:T(128)S(1)}, s32[4]{0:T(128)}, u32[]{:S(2)}) copy-start(s32[4]{0:T(128)} %lengths.3) | copy-start | bytes 52
  20.0 17.8 %copy-start.4 = (s32[8]{0:T(128)S(1)}, s32[8]{0:T(128)}, u32[]{:S(2)}) copy-start(s32[8]{0:T(128)} %counts.3) | copy-start | bytes 100
  20.0 16.7 %collective-permute-start.19 = (bf16[512,128]{1,0:T(8,128)(2,1)S(1)}, bf16[512,128]{1,0:T(8,128)(2,1)S(1)}, u32[]{:S(2)}, u32[]{:S(2)}) collective-permute-start(bf16[512,128]{1,0:T(8,128)(2,1)S(1)} %collective-permute-done.15), channel_id=1, source_target_pairs={{0,4},{1,5},{2,6},{3,7},{4,0},{5,1},{6,2},{7,3},{8,12},{9,13},{10,... | collective-permute-start | bytes 393224 | tf_op jit(solution)/shard_map/ppermute | solution.py:334
  20.3 16.5 %collective-permute-start.21 = (bf16[512,128]{1,0:T(8,128)(2,1)S(1)}, bf16[512,128]{1,0:T(8,128)(2,1)S(1)}, u32[]{:S(2)}, u32[]{:S(2)}) collective-permute-start(bf16[512,128]{1,0:T(8,128)(2,1)S(1)} %collective-permute-done.15), channel_id=1, source_target_pairs={{0,6},{1,7},{2,4},{3,5},{4,2},{5,3},{6,0},{7,1},{8,14},{9,15},{10,... | collective-permute-start | bytes 393224 | tf_op jit(solution)/shard_map/ppermute | solution.py:334
  23.8 13.5 %collective-permute-start.26 = (bf16[512,128]{1,0:T(8,128)(2,1)S(1)}, bf16[512,128]{1,0:T(8,128)(2,1)S(1)}, u32[]{:S(2)}, u32[]{:S(2)}) collective-permute-start(bf16[512,128]{1,0:T(8,128)(2,1)S(1)} %collective-permute-done.25.refs_2_), channel_id=1, source_target_pairs={{0,1},{1,0},{2,3},{3,2},{4,5},{5,4},{6,7},{7,6},{8,9},{9,8},{10,11... | collective-permute-start | bytes 393224 | tf_op jit(solution)/shard_map/ppermute | solution.py:334
  26.8 10.6 %collective-permute-start.28 = (bf16[512,128]{1,0:T(8,128)(2,1)S(1)}, bf16[512,128]{1,0:T(8,128)(2,1)S(1)}, u32[]{:S(2)}, u32[]{:S(2)}) collective-permute-start(bf16[512,128]{1,0:T(8,128)(2,1)S(1)} %collective-permute-done.27.refs_4_), channel_id=1, source_target_pairs={{0,1},{1,0},{2,3},{3,2},{4,5},{5,4},{6,7},{7,6},{8,9},{9,8},{10,11... | collective-permute-start | bytes 393224 | tf_op jit(solution)/shard_map/ppermute | solution.py:334
  27.5 10.3 %collective-permute-start.30 = (bf16[512,128]{1,0:T(8,128)(2,1)S(1)}, bf16[512,128]{1,0:T(8,128)(2,1)S(1)}, u32[]{:S(2)}, u32[]{:S(2)}) collective-permute-start(bf16[512,128]{1,0:T(8,128)(2,1)S(1)} %collective-permute-done.29.refs_6_), channel_id=1, source_target_pairs={{0,1},{1,0},{2,3},{3,2},{4,5},{5,4},{6,7},{7,6},{8,9},{9,8},{10,11... | collective-permute-start | bytes 393224 | tf_op jit(solution)/shard_map/ppermute | solution.py:334
  36.7 10.1 %collective-permute-start.16 = (bf16[512,128]{1,0:T(8,128)(2,1)S(1)}, bf16[512,128]{1,0:T(8,128)(2,1)S(1)}, u32[]{:S(2)}, u32[]{:S(2)}) collective-permute-start(bf16[512,128]{1,0:T(8,128)(2,1)S(1)} %collective-permute-done.15), channel_id=1, source_target_pairs={{0,1},{1,0},{2,3},{3,2},{4,5},{5,4},{6,7},{7,6},{8,9},{9,8},{10,11... | collective-permute-start | bytes 393224 | tf_op jit(solution)/shard_map/ppermute | solution.py:334
  36.8 10.0 %collective-permute-start.18 = (bf16[512,128]{1,0:T(8,128)(2,1)S(1)}, bf16[512,128]{1,0:T(8,128)(2,1)S(1)}, u32[]{:S(2)}, u32[]{:S(2)}) collective-permute-start(bf16[512,128]{1,0:T(8,128)(2,1)S(1)} %collective-permute-done.17), channel_id=1, source_target_pairs={{0,1},{1,0},{2,3},{3,2},{4,5},{5,4},{6,7},{7,6},{8,9},{9,8},{10,11... | collective-permute-start | bytes 393224 | tf_op jit(solution)/shard_map/ppermute | solution.py:334
  37.3 9.5 %collective-permute-start.20 = (bf16[512,128]{1,0:T(8,128)(2,1)S(1)}, bf16[512,128]{1,0:T(8,128)(2,1)S(1)}, u32[]{:S(2)}, u32[]{:S(2)}) collective-permute-start(bf16[512,128]{1,0:T(8,128)(2,1)S(1)} %collective-permute-done.19), channel_id=1, source_target_pairs={{0,1},{1,0},{2,3},{3,2},{4,5},{5,4},{6,7},{7,6},{8,9},{9,8},{10,11... | collective-permute-start | bytes 393224 | tf_op jit(solution)/shard_map/ppermute | solution.py:334
  37.4 9.5 %collective-permute-start.22 = (bf16[512,128]{1,0:T(8,128)(2,1)S(1)}, bf16[512,128]{1,0:T(8,128)(2,1)S(1)}, u32[]{:S(2)}, u32[]{:S(2)}) collective-permute-start(bf16[512,128]{1,0:T(8,128)(2,1)S(1)} %collective-permute-done.21), channel_id=1, source_target_pairs={{0,1},{1,0},{2,3},{3,2},{4,5},{5,4},{6,7},{7,6},{8,9},{9,8},{10,11... | collective-permute-start | bytes 393224 | tf_op jit(solution)/shard_map/ppermute | solution.py:334
  48.6 0.8 %copy-start.5 = (bf16[1024,256]{1,0:T(8,128)(2,1)}, bf16[1024,256]{1,0:T(8,128)(2,1)S(1)}, u32[]{:S(2)}) copy-start(bf16[1024,256]{1,0:T(8,128)(2,1)S(1)} %get-tuple-element.169) | copy-start | bytes 1572868
where the time goes:
time: 49.6 us; the launch traced here: 49.4 us
  starting transfers between devices  22.9 us (46%)
  Pallas kernels  18.3 us (37%)
  waiting for transfers between devices  4.71 us (9%)
  local copies, waits for them, and re-layouts  2.48 us (5%)
  between operations  0.79 us (2%)
    ppermute x23, starting transfers between devices, moved(): return lax.ppermute(value, AXES, pairs)  22.9 us
    pallas_call x3, Pallas kernels, attend(): pl.pallas_call(functools.partial(attend_kernel, (delta, tiles, heads, til...  18.1 us
    ppermute x23, waiting for transfers between devices, moved(): return lax.ppermute(value, AXES, pairs)  4.71 us
    unnamed x12, local copies, waits for them, and re-layouts  2.48 us
  transfers between devices with their start and end apart: 23, of which 3 were waited for; matrix products, arithmetic and copies ran while one was open for 0% of the time, Pallas kernels for 34%

commit v1 on v0

--- a/solution.py
+++ b/solution.py
@@ -33,7 +33,7 @@
     return pl.pallas_call(
         join_kernel,
         out_shape=jax.ShapeDtypeStruct((2 * rows, dim), keys.dtype),
-        in_specs=[pl.BlockSpec(memory_space=pl.ANY)] * 2,
+        in_specs=[pl.BlockSpec(memory_space=pltpu.MemorySpace.HBM)] * 2,
         out_specs=pl.BlockSpec(memory_space=pltpu.VMEM),
         scratch_shapes=[pltpu.SemaphoreType.DMA((2,))],
         compiler_params=pltpu.CompilerParams(vmem_limit_bytes=4 << 20),
@@ -54,7 +54,7 @@
     else:
         top_all, acc_all = refs[2:4]
         refs = refs[4:]
-    k_all, v_all, score_a, score_b, top, acc, starts, work = refs
+    k_all, v_all, score_a, score_b, top, acc, opened, starts, work = refs
     rows = q_ref.shape[0]
     dim = k_all.shape[2]
     tile_k = k_all.shape[1]
@@ -112,7 +112,6 @@
         query_start = own_start + row
         query_end = query_start + tile_q - 1
         opened_low = opening(query_start)
-        opened_high = opening(query_end)
 
         def plan_keys(tile, carry):
             count, opener = carry
@@ -130,7 +129,7 @@
                 & (key_start <= query_end)
                 & (key_end >= opened_low)
             )
-            whole = (key_end <= query_start) & (key_start >= opened_high)
+            whole = (key_end <= query_start) & (key_start >= opening(key_end))
             at = count * FIELDS
             work[at] = index
             work[at + 1] = tile
@@ -182,6 +181,16 @@
 
         @pl.when(work[base + 4] == 1)
         def _():
+            row = own_start + query_index * tile_q
+            position = row + lax.broadcasted_iota(jnp.int32, (tile_q, dim), 0)
+
+            def look(index, edge):
+                edge = edge + lengths[index]
+                opened[...] = jnp.where(position >= edge, edge, opened[...])
+                return edge
+
+            opened[...] = jnp.zeros((tile_q, dim), jnp.int32)
+            lax.fori_loop(0, documents, look, jnp.int32(0))
             if first:
                 top[...] = jnp.full(top.shape, NEGATIVE, jnp.float32)
                 acc[...] = jnp.zeros(acc.shape, jnp.float32)
@@ -191,32 +200,29 @@
 
         def run(masked):
             v_tile = v_all[work[base + 1]]
+            key_start = work[base + 3]
+            begin = opened[...]
             if masked:
                 row = own_start + query_index * tile_q
-                narrow = row + lax.broadcasted_iota(jnp.int32, (tile_q, dim), 0)
-
-                def look(index, carry):
-                    edge, begin = carry
-                    edge = edge + lengths[index]
-                    return edge, jnp.where(narrow >= edge, edge, begin)
-
-                opened = lax.fori_loop(
-                    0, documents, look, (jnp.int32(0), jnp.zeros((tile_q, dim), jnp.int32))
-                )[1]
-                key_position = work[base + 3] + lax.broadcasted_iota(
-                    jnp.int32, (tile_q, tile_k), 1
-                )
-                visible = (key_position <= wide(narrow, tile_k // dim)) & (
-                    key_position >= wide(opened, tile_k // dim)
-                )
+                position = row + lax.broadcasted_iota(jnp.int32, (tile_q, dim), 0)
+                behind = wide((position - begin).astype(jnp.uint32), tile_k // dim)
+                key_position = key_start + lax.broadcasted_iota(jnp.int32, (1, tile_k), 1)
+            else:
+                seen = begin <= key_start
             for head in range(heads):
                 coming[head] = score(item + 1, head)
                 scores = current[head]
+                before = top[head]
                 if masked:
-                    scores = jnp.where(visible, scores, NEGATIVE)
-                before = top[head]
-                after = jnp.maximum(before, jnp.max(scores, axis=1, keepdims=True))
-                weights = jnp.exp2((scores - wide(after, tile_k // dim)) * scale)
+                    into = (key_position - wide(begin, tile_k // dim)).astype(jnp.uint32)
+                    scores = jnp.where(into <= behind, scores, NEGATIVE)
+                    after = jnp.maximum(before, jnp.max(scores, axis=1, keepdims=True))
+                    taken = after
+                else:
+                    after = jnp.maximum(before, jnp.max(scores, axis=1, keepdims=True))
+                    after = jnp.where(seen, after, before)
+                    taken = jnp.where(seen, after, -NEGATIVE)
+                weights = jnp.exp2((scores - wide(taken, tile_k // dim)) * scale)
                 factor = jnp.exp2((before - after) * scale)
                 top[head] = after
                 acc[head] = acc[head] * wide(factor, 2) + jnp.dot(
@@ -276,6 +282,7 @@
         pltpu.VMEM((heads, tile_q, tile_k), jnp.float32),
         pltpu.VMEM(top, jnp.float32),
         pltpu.VMEM(acc, jnp.float32),
+        pltpu.VMEM((tile_q, dim), jnp.int32),
         pltpu.SMEM((counts.shape[0] + 1,), jnp.int32),
         pltpu.SMEM((FIELDS * (steps * tiles + 2),), jnp.int32),
     ]

time: 49.6 us -> 50.5 us (1.018)
  Pallas kernels: 18.3 us -> 19.1 us
    pallas_call x3, Pallas kernels: 18.1 us -> 19 us  [attend(): pl.pallas_call(functools.partial(attend_kernel, (delta, tiles, heads, til...]
where the time goes in v1:
time: 50.5 us; the launch traced here: 50.3 us
  starting transfers between devices  22.9 us (45%)
  Pallas kernels  19.1 us (38%)
  waiting for transfers between devices  4.71 us (9%)
  local copies, waits for them, and re-layouts  2.48 us (5%)
  between operations  0.78 us (2%)
    ppermute x23, starting transfers between devices, moved(): return lax.ppermute(value, AXES, pairs)  22.9 us
    pallas_call x3, Pallas kernels, attend(): pl.pallas_call(functools.partial(attend_kernel, (delta, tiles, heads, til...  19 us
    ppermute x23, waiting for transfers between devices, moved(): return lax.ppermute(value, AXES, pairs)  4.71 us
    unnamed x12, local copies, waits for them, and re-layouts  2.48 us
  transfers between devices with their start and end apart: 23, of which 3 were waited for; matrix products, arithmetic and copies ran while one was open for 0% of the time, Pallas kernels for 34%

profile of v1, /device:TPU:11, one launch (start us, length us, event | category | flops | bytes accessed | tf_op | source)
XLA Modules:
  0.0 50.3 jit_solution(3648880637554638389)
XLA Ops:
  0.0 0.8 %copy-done = bf16[256,128]{1,0:T(8,128)(2,1)S(1)} copy-done((bf16[256,128]{1,0:T(8,128)(2,1)S(1)}, bf16[256,128]{1,0:T(8,128)(2,1)}, u32[]{:S(2)}) %copy-start) | copy-done | bytes 65560
  0.8 0.8 %copy-done.1 = bf16[256,128]{1,0:T(8,128)(2,1)S(1)} copy-done((bf16[256,128]{1,0:T(8,128)(2,1)S(1)}, bf16[256,128]{1,0:T(8,128)(2,1)}, u32[]{:S(2)}) %copy-start.1) | copy-done | bytes 65560
  1.7 0.2 join.1.refs_0_
  1.8 1.3 %collective-permute-start.9 = (bf16[512,128]{1,0:T(8,128)(2,1)S(1)}, bf16[512,128]{1,0:T(8,128)(2,1)S(1)}, u32[]{:S(2)}, u32[]{:S(2)}) collective-permute-start(bf16[512,128]{1,0:T(8,128)(2,1)S(1)} %join.1.refs_0_), channel_id=1, source_target_pairs={{0,2},{1,3},{2,0},{3,1},{4,6},{5,7},{6,4},{7,5},{8,10},{9,11},{10,... | collective-permute-start | bytes 393224 | tf_op jit(solution)/shard_map/ppermute | solution.py:341
  3.1 0.3 collective-permute-start.11
  3.4 1.2 %collective-permute-start.13 = (bf16[512,128]{1,0:T(8,128)(2,1)S(1)}, bf16[512,128]{1,0:T(8,128)(2,1)S(1)}, u32[]{:S(2)}, u32[]{:S(2)}) collective-permute-start(bf16[512,128]{1,0:T(8,128)(2,1)S(1)} %join.1.refs_0_), channel_id=1, source_target_pairs={{0,6},{1,7},{2,4},{3,5},{4,2},{5,3},{6,0},{7,1},{8,14},{9,15},{10,... | collective-permute-start | bytes 393224 | tf_op jit(solution)/shard_map/ppermute | solution.py:341
  4.6 1.5 %collective-permute-start.8 = (bf16[512,128]{1,0:T(8,128)(2,1)S(1)}, bf16[512,128]{1,0:T(8,128)(2,1)S(1)}, u32[]{:S(2)}, u32[]{:S(2)}) collective-permute-start(bf16[512,128]{1,0:T(8,128)(2,1)S(1)} %join.1.refs_0_), channel_id=1, source_target_pairs={{0,1},{1,0},{2,3},{3,2},{4,5},{5,4},{6,7},{7,6},{8,9},{9,8},{10,11... | collective-permute-start | bytes 393224 | tf_op jit(solution)/shard_map/ppermute | solution.py:341
  6.1 1.3 %collective-permute-start.23 = (bf16[512,128]{1,0:T(8,128)(2,1)S(1)}, bf16[512,128]{1,0:T(8,128)(2,1)S(1)}, u32[]{:S(2)}, u32[]{:S(2)}) collective-permute-start(bf16[512,128]{1,0:T(8,128)(2,1)S(1)} %join.1.refs_0_), channel_id=1, source_target_pairs={{0,8},{1,9},{2,10},{3,11},{4,12},{5,13},{6,14},{7,15},{8,16},{9,17... | collective-permute-start | bytes 393224 | tf_op jit(solution)/shard_map/ppermute | solution.py:341
  7.4 1.2 %collective-permute-start.15 = (bf16[512,128]{1,0:T(8,128)(2,1)S(1)}, bf16[512,128]{1,0:T(8,128)(2,1)S(1)}, u32[]{:S(2)}, u32[]{:S(2)}) collective-permute-start(bf16[512,128]{1,0:T(8,128)(2,1)S(1)} %join.1.refs_0_), channel_id=1, source_target_pairs={{0,16},{1,17},{2,18},{3,19},{4,20},{5,21},{6,22},{7,23},{8,24},{9,... | collective-permute-start | bytes 393224 | tf_op jit(solution)/shard_map/ppermute | solution.py:341
  8.6 0.0 collective-permute-done.11.refs_4_
  8.6 2.0 %collective-permute-start.10 = (bf16[512,128]{1,0:T(8,128)(2,1)S(1)}, bf16[512,128]{1,0:T(8,128)(2,1)S(1)}, u32[]{:S(2)}, u32[]{:S(2)}) collective-permute-start(bf16[512,128]{1,0:T(8,128)(2,1)S(1)} %collective-permute-done.9.refs_2_), channel_id=1, source_target_pairs={{0,1},{1,0},{2,3},{3,2},{4,5},{5,4},{6,7},{7,6},{8,9},{9,8},{10,11... | collective-permute-start | bytes 393224 | tf_op jit(solution)/shard_map/ppermute | solution.py:341
  10.6 0.0 collective-permute-done.13.refs_6_
  10.6 1.2 %collective-permute-start.12 = (bf16[512,128]{1,0:T(8,128)(2,1)S(1)}, bf16[512,128]{1,0:T(8,128)(2,1)S(1)}, u32[]{:S(2)}, u32[]{:S(2)}) collective-permute-start(bf16[512,128]{1,0:T(8,128)(2,1)S(1)} %collective-permute-done.11.refs_4_), channel_id=1, source_target_pairs={{0,1},{1,0},{2,3},{3,2},{4,5},{5,4},{6,7},{7,6},{8,9},{9,8},{10,11... | collective-permute-start | bytes 393224 | tf_op jit(solution)/shard_map/ppermute | solution.py:341
  11.8 0.0 collective-permute-done.8.refs_1_
  11.8 0.0 collective-permute-start.14
  11.8 0.0 collective-permute-done.23.refs_0_
  11.8 1.3 %collective-permute-start.25 = (bf16[512,128]{1,0:T(8,128)(2,1)S(1)}, bf16[512,128]{1,0:T(8,128)(2,1)S(1)}, u32[]{:S(2)}, u32[]{:S(2)}) collective-permute-start(bf16[512,128]{1,0:T(8,128)(2,1)S(1)} %collective-permute-done.23.refs_0_), channel_id=1, source_target_pairs={{0,2},{1,3},{2,0},{3,1},{4,6},{5,7},{6,4},{7,5},{8,10},{9,11},{10,... | collective-permute-start | bytes 393224 | tf_op jit(solution)/shard_map/ppermute | solution.py:341
  13.1 2.7 %collective-permute-done.15 = bf16[512,128]{1,0:T(8,128)(2,1)S(1)} collective-permute-done((bf16[512,128]{1,0:T(8,128)(2,1)S(1)}, bf16[512,128]{1,0:T(8,128)(2,1)S(1)}, u32[]{:S(2)}, u32[]{:S(2)}) %collective-permute-start.15) | collective-permute-done | bytes 131104 | tf_op jit(solution)/shard_map/ppermute | solution.py:341
  15.8 0.3 collective-permute-start.27
  16.1 0.0 collective-permute-done.10.refs_3_
  16.1 2.2 %collective-permute-start.29 = (bf16[512,128]{1,0:T(8,128)(2,1)S(1)}, bf16[512,128]{1,0:T(8,128)(2,1)S(1)}, u32[]{:S(2)}, u32[]{:S(2)}) collective-permute-start(bf16[512,128]{1,0:T(8,128)(2,1)S(1)} %collective-permute-done.23.refs_0_), channel_id=1, source_target_pairs={{0,6},{1,7},{2,4},{3,5},{4,2},{5,3},{6,0},{7,1},{8,14},{9,15},{10,... | collective-permute-start | bytes 393224 | tf_op jit(solution)/shard_map/ppermute | solution.py:341
  18.3 0.0 collective-permute-done.12.refs_5_
  18.3 1.4 %collective-permute-start.24 = (bf16[512,128]{1,0:T(8,128)(2,1)S(1)}, bf16[512,128]{1,0:T(8,128)(2,1)S(1)}, u32[]{:S(2)}, u32[]{:S(2)}) collective-permute-start(bf16[512,128]{1,0:T(8,128)(2,1)S(1)} %collective-permute-done.23.refs_0_), channel_id=1, source_target_pairs={{0,1},{1,0},{2,3},{3,2},{4,5},{5,4},{6,7},{7,6},{8,9},{9,8},{10,11... | collective-permute-start | bytes 393224 | tf_op jit(solution)/shard_map/ppermute | solution.py:341
  19.7 0.2 collective-permute-start.17
  19.9 0.1 pad_add_fusion.place
  20.0 0.0 collective-permute-done.25.refs_2_
  20.0 0.3 collective-permute-start.19
  20.3 0.0 collective-permute-done.27.refs_4_
  20.3 2.2 %collective-permute-start.21 = (bf16[512,128]{1,0:T(8,128)(2,1)S(1)}, bf16[512,128]{1,0:T(8,128)(2,1)S(1)}, u32[]{:S(2)}, u32[]{:S(2)}) collective-permute-start(bf16[512,128]{1,0:T(8,128)(2,1)S(1)} %collective-permute-done.15), channel_id=1, source_target_pairs={{0,6},{1,7},{2,4},{3,5},{4,2},{5,3},{6,0},{7,1},{8,14},{9,15},{10,... | collective-permute-start | bytes 393224 | tf_op jit(solution)/shard_map/ppermute | solution.py:341
  22.5 1.3 %collective-permute-done.29.refs_6_ = bf16[512,128]{1,0:T(8,128)(2,1)S(1)} collective-permute-done((bf16[512,128]{1,0:T(8,128)(2,1)S(1)}, bf16[512,128]{1,0:T(8,128)(2,1)S(1)}, u32[]{:S(2)}, u32[]{:S(2)}) %collective-permute-start.29) | collective-permute-done | bytes 131104 | tf_op jit(solution)/shard_map/ppermute | solution.py:341
  23.8 3.0 %collective-permute-start.26 = (bf16[512,128]{1,0:T(8,128)(2,1)S(1)}, bf16[512,128]{1,0:T(8,128)(2,1)S(1)}, u32[]{:S(2)}, u32[]{:S(2)}) collective-permute-start(bf16[512,128]{1,0:T(8,128)(2,1)S(1)} %collective-permute-done.25.refs_2_), channel_id=1, source_target_pairs={{0,1},{1,0},{2,3},{3,2},{4,5},{5,4},{6,7},{7,6},{8,9},{9,8},{10,11... | collective-permute-start | bytes 393224 | tf_op jit(solution)/shard_map/ppermute | solution.py:341
  26.8 0.0 collective-permute-done.24.refs_1_
  26.8 0.0 collective-permute-start.28
  26.8 0.6 %collective-permute-done.17 = bf16[512,128]{1,0:T(8,128)(2,1)S(1)} collective-permute-done((bf16[512,128]{1,0:T(8,128)(2,1)S(1)}, bf16[512,128]{1,0:T(8,128)(2,1)S(1)}, u32[]{:S(2)}, u32[]{:S(2)}) %collective-permute-start.17) | collective-permute-done | bytes 131104 | tf_op jit(solution)/shard_map/ppermute | solution.py:341
  27.5 0.9 %collective-permute-start.30 = (bf16[512,128]{1,0:T(8,128)(2,1)S(1)}, bf16[512,128]{1,0:T(8,128)(2,1)S(1)}, u32[]{:S(2)}, u32[]{:S(2)}) collective-permute-start(bf16[512,128]{1,0:T(8,128)(2,1)S(1)} %collective-permute-done.29.refs_6_), channel_id=1, source_target_pairs={{0,1},{1,0},{2,3},{3,2},{4,5},{5,4},{6,7},{7,6},{8,9},{9,8},{10,11... | collective-permute-start | bytes 393224 | tf_op jit(solution)/shard_map/ppermute | solution.py:341
  28.4 7.9 %shard_map.57 = (f32[2,2,512,128]{3,2,1,0:T(8,128)S(1)}, f32[2,2,512,256]{3,2,1,0:T(8,128)S(1)}, s32[1]{0:T(128)}) custom-call(s32[2]{0:T(128)S(1)} %pad_add_fusion.place, s32[4]{0:T(128)} %lengths.3, s32[8]{0:T(128)} %counts.3, bf16[1024,256]{1,0:T(8,128)(2,1)} %q_ref.3, bf16[512,128]{1,0:T(8,128)(2,1)S(1)} %join.1.refs_0_, ...), custom_call_target="tpu_custom_call" | custom-call | flops 2147483648 | bytes 4194304 | tf_op jit(solution)/shard_map/pallas_call | solution.py:306
  37.0 0.0 collective-permute-done.19
  37.0 0.1 collective-permute-start.16
  37.1 0.5 collective-permute-start.18
  37.5 0.0 collective-permute-done.26.refs_3_
  37.5 0.1 collective-permute-start.20
  37.6 0.0 collective-permute-done.28.refs_5_
  37.6 0.4 collective-permute-start.22
  38.1 9.4 %shard_map.58 = (f32[2,2,512,128]{3,2,1,0:T(8,128)S(1)}, f32[2,2,512,256]{3,2,1,0:T(8,128)S(1)}) custom-call(s32[2]{0:T(128)S(1)} %pad_add_fusion.place, s32[4]{0:T(128)S(1)} %copy-done.3, s32[8]{0:T(128)S(1)} %copy-done.4, bf16[1024,256]{1,0:T(8,128)(2,1)S(1)} %copy-done.2, ...), custom_call_target="tpu_custom_call", output_to_operand_aliasing={{0}: (12, {}), {1}: (13, {})} | custom-call | flops 2147483648 | bytes 4194304 | tf_op jit(solution)/shard_map/pallas_call | solution.py:306
  47.6 1.9 %conditional.1 = (bf16[1024,256]{1,0:T(8,128)(2,1)S(1)}) conditional(s32[]{:T(128)} %bitcast.2, (s32[2]{0:T(128)S(1)}, s32[4]{0:T(128)S(1)}, s32[8]{0:T(128)S(1)}, bf16[1024,256]{1,0:T(8,128)(2,1)S(1)}, bf16[512,128]{1,0:T(8,128)(2,1)S(1)}, /*index=5*/bf16[512,128]{1,0:T(8,128)(2,1)S(1)}, bf16[512,128]{1,0:T(8,128)(2,1)S(1)}, ...), branch_computations={%region_0.0_spmd, %region_1.0_spmd} | conditional | flops 4294967296 | bytes 12583240 | solution.py:399
  47.6 1.7 %branch_0_fun.1 = bf16[1024,256]{1,0:T(8,128)(2,1)S(1)} custom-call(s32[2]{0:T(128)S(1)} %get-tuple-element.64.place, s32[4]{0:T(128)S(1)} %get-tuple-element.65.lengths, s32[8]{0:T(128)S(1)} %get-tuple-element.66.counts, bf16[1024,256]{1,0:T(8,128)(2,1)S(1)} %get-tuple-element.67.q_ref, bf16[512,128]{1,0:T(8,128)(2,1)S(1)} %get-tuple-element.68.refs_0_, ...), custom_call_target="tpu_custom_call" | custom-call | flops 2147483648 | bytes 4194304 | tf_op jit(solution)/shard_map/cond/branch_0_fun/pallas_call | solution.py:306
  49.5 0.0 copy-start.5
  49.5 0.8 %copy-done.5 = bf16[1024,256]{1,0:T(8,128)(2,1)} copy-done((bf16[1024,256]{1,0:T(8,128)(2,1)}, bf16[1024,256]{1,0:T(8,128)(2,1)S(1)}, u32[]{:S(2)}) %copy-start.5) | copy-done | bytes 524312
  (16 shorter events, 0.0 us)
Async XLA Ops:
  0.0 0.8 %copy-start = (bf16[256,128]{1,0:T(8,128)(2,1)S(1)}, bf16[256,128]{1,0:T(8,128)(2,1)}, u32[]{:S(2)}) copy-start(bf16[256,128]{1,0:T(8,128)(2,1)} %keys.1) | copy-start | bytes 196612
  0.8 0.8 %copy-start.1 = (bf16[256,128]{1,0:T(8,128)(2,1)S(1)}, bf16[256,128]{1,0:T(8,128)(2,1)}, u32[]{:S(2)}) copy-start(bf16[256,128]{1,0:T(8,128)(2,1)} %values.1) | copy-start | bytes 196612
  1.8 5.5 %collective-permute-start.9 = (bf16[512,128]{1,0:T(8,128)(2,1)S(1)}, bf16[512,128]{1,0:T(8,128)(2,1)S(1)}, u32[]{:S(2)}, u32[]{:S(2)}) collective-permute-start(bf16[512,128]{1,0:T(8,128)(2,1)S(1)} %join.1.refs_0_), channel_id=1, source_target_pairs={{0,2},{1,3},{2,0},{3,1},{4,6},{5,7},{6,4},{7,5},{8,10},{9,11},{10,... | collective-permute-start | bytes 393224 | tf_op jit(solution)/shard_map/ppermute | solution.py:341
  3.1 5.5 %collective-permute-start.11 = (bf16[512,128]{1,0:T(8,128)(2,1)S(1)}, bf16[512,128]{1,0:T(8,128)(2,1)S(1)}, u32[]{:S(2)}, u32[]{:S(2)}) collective-permute-start(bf16[512,128]{1,0:T(8,128)(2,1)S(1)} %join.1.refs_0_), channel_id=1, source_target_pairs={{0,4},{1,5},{2,6},{3,7},{4,0},{5,1},{6,2},{7,3},{8,12},{9,13},{10,... | collective-permute-start | bytes 393224 | tf_op jit(solution)/shard_map/ppermute | solution.py:341
  3.4 7.2 %collective-permute-start.13 = (bf16[512,128]{1,0:T(8,128)(2,1)S(1)}, bf16[512,128]{1,0:T(8,128)(2,1)S(1)}, u32[]{:S(2)}, u32[]{:S(2)}) collective-permute-start(bf16[512,128]{1,0:T(8,128)(2,1)S(1)} %join.1.refs_0_), channel_id=1, source_target_pairs={{0,6},{1,7},{2,4},{3,5},{4,2},{5,3},{6,0},{7,1},{8,14},{9,15},{10,... | collective-permute-start | bytes 393224 | tf_op jit(solution)/shard_map/ppermute | solution.py:341
  4.6 7.3 %collective-permute-start.8 = (bf16[512,128]{1,0:T(8,128)(2,1)S(1)}, bf16[512,128]{1,0:T(8,128)(2,1)S(1)}, u32[]{:S(2)}, u32[]{:S(2)}) collective-permute-start(bf16[512,128]{1,0:T(8,128)(2,1)S(1)} %join.1.refs_0_), channel_id=1, source_target_pairs={{0,1},{1,0},{2,3},{3,2},{4,5},{5,4},{6,7},{7,6},{8,9},{9,8},{10,11... | collective-permute-start | bytes 393224 | tf_op jit(solution)/shard_map/ppermute | solution.py:341
  6.1 5.8 %collective-permute-start.23 = (bf16[512,128]{1,0:T(8,128)(2,1)S(1)}, bf16[512,128]{1,0:T(8,128)(2,1)S(1)}, u32[]{:S(2)}, u32[]{:S(2)}) collective-permute-start(bf16[512,128]{1,0:T(8,128)(2,1)S(1)} %join.1.refs_0_), channel_id=1, source_target_pairs={{0,8},{1,9},{2,10},{3,11},{4,12},{5,13},{6,14},{7,15},{8,16},{9,17... | collective-permute-start | bytes 393224 | tf_op jit(solution)/shard_map/ppermute | solution.py:341
  7.4 8.5 %collective-permute-start.15 = (bf16[512,128]{1,0:T(8,128)(2,1)S(1)}, bf16[512,128]{1,0:T(8,128)(2,1)S(1)}, u32[]{:S(2)}, u32[]{:S(2)}) collective-permute-start(bf16[512,128]{1,0:T(8,128)(2,1)S(1)} %join.1.refs_0_), channel_id=1, source_target_pairs={{0,16},{1,17},{2,18},{3,19},{4,20},{5,21},{6,22},{7,23},{8,24},{9,... | collective-permute-start | bytes 393224 | tf_op jit(solution)/shard_map/ppermute | solution.py:341
  8.6 7.5 %collective-permute-start.10 = (bf16[512,128]{1,0:T(8,128)(2,1)S(1)}, bf16[512,128]{1,0:T(8,128)(2,1)S(1)}, u32[]{:S(2)}, u32[]{:S(2)}) collective-permute-start(bf16[512,128]{1,0:T(8,128)(2,1)S(1)} %collective-permute-done.9.refs_2_), channel_id=1, source_target_pairs={{0,1},{1,0},{2,3},{3,2},{4,5},{5,4},{6,7},{7,6},{8,9},{9,8},{10,11... | collective-permute-start | bytes 393224 | tf_op jit(solution)/shard_map/ppermute | solution.py:341
  10.6 7.6 %collective-permute-start.12 = (bf16[512,128]{1,0:T(8,128)(2,1)S(1)}, bf16[512,128]{1,0:T(8,128)(2,1)S(1)}, u32[]{:S(2)}, u32[]{:S(2)}) collective-permute-start(bf16[512,128]{1,0:T(8,128)(2,1)S(1)} %collective-permute-done.11.refs_4_), channel_id=1, source_target_pairs={{0,1},{1,0},{2,3},{3,2},{4,5},{5,4},{6,7},{7,6},{8,9},{9,8},{10,11... | collective-permute-start | bytes 393224 | tf_op jit(solution)/shard_map/ppermute | solution.py:341
  11.8 7.9 %collective-permute-start.14 = (bf16[512,128]{1,0:T(8,128)(2,1)S(1)}, bf16[512,128]{1,0:T(8,128)(2,1)S(1)}, u32[]{:S(2)}, u32[]{:S(2)}) collective-permute-start(bf16[512,128]{1,0:T(8,128)(2,1)S(1)} %collective-permute-done.13.refs_6_), channel_id=1, source_target_pairs={{0,1},{1,0},{2,3},{3,2},{4,5},{5,4},{6,7},{7,6},{8,9},{9,8},{10,11... | collective-permute-start | bytes 393224 | tf_op jit(solution)/shard_map/ppermute | solution.py:341
  11.8 8.2 %collective-permute-start.25 = (bf16[512,128]{1,0:T(8,128)(2,1)S(1)}, bf16[512,128]{1,0:T(8,128)(2,1)S(1)}, u32[]{:S(2)}, u32[]{:S(2)}) collective-permute-start(bf16[512,128]{1,0:T(8,128)(2,1)S(1)} %collective-permute-done.23.refs_0_), channel_id=1, source_target_pairs={{0,2},{1,3},{2,0},{3,1},{4,6},{5,7},{6,4},{7,5},{8,10},{9,11},{10,... | collective-permute-start | bytes 393224 | tf_op jit(solution)/shard_map/ppermute | solution.py:341
  15.8 4.5 %collective-permute-start.27 = (bf16[512,128]{1,0:T(8,128)(2,1)S(1)}, bf16[512,128]{1,0:T(8,128)(2,1)S(1)}, u32[]{:S(2)}, u32[]{:S(2)}) collective-permute-start(bf16[512,128]{1,0:T(8,128)(2,1)S(1)} %collective-permute-done.23.refs_0_), channel_id=1, source_target_pairs={{0,4},{1,5},{2,6},{3,7},{4,0},{5,1},{6,2},{7,3},{8,12},{9,13},{10,... | collective-permute-start | bytes 393224 | tf_op jit(solution)/shard_map/ppermute | solution.py:341
  16.1 7.7 %collective-permute-start.29 = (bf16[512,128]{1,0:T(8,128)(2,1)S(1)}, bf16[512,128]{1,0:T(8,128)(2,1)S(1)}, u32[]{:S(2)}, u32[]{:S(2)}) collective-permute-start(bf16[512,128]{1,0:T(8,128)(2,1)S(1)} %collective-permute-done.23.refs_0_), channel_id=1, source_target_pairs={{0,6},{1,7},{2,4},{3,5},{4,2},{5,3},{6,0},{7,1},{8,14},{9,15},{10,... | collective-permute-start | bytes 393224 | tf_op jit(solution)/shard_map/ppermute | solution.py:341
  18.3 8.6 %collective-permute-start.24 = (bf16[512,128]{1,0:T(8,128)(2,1)S(1)}, bf16[512,128]{1,0:T(8,128)(2,1)S(1)}, u32[]{:S(2)}, u32[]{:S(2)}) collective-permute-start(bf16[512,128]{1,0:T(8,128)(2,1)S(1)} %collective-permute-done.23.refs_0_), channel_id=1, source_target_pairs={{0,1},{1,0},{2,3},{3,2},{4,5},{5,4},{6,7},{7,6},{8,9},{9,8},{10,11... | collective-permute-start | bytes 393224 | tf_op jit(solution)/shard_map/ppermute | solution.py:341
  19.7 7.8 %collective-permute-start.17 = (bf16[512,128]{1,0:T(8,128)(2,1)S(1)}, bf16[512,128]{1,0:T(8,128)(2,1)S(1)}, u32[]{:S(2)}, u32[]{:S(2)}) collective-permute-start(bf16[512,128]{1,0:T(8,128)(2,1)S(1)} %collective-permute-done.15), channel_id=1, source_target_pairs={{0,2},{1,3},{2,0},{3,1},{4,6},{5,7},{6,4},{7,5},{8,10},{9,11},{10,... | collective-permute-start | bytes 393224 | tf_op jit(solution)/shard_map/ppermute | solution.py:341
  20.0 18.1 %copy-start.2 = (bf16[1024,256]{1,0:T(8,128)(2,1)S(1)}, bf16[1024,256]{1,0:T(8,128)(2,1)}, u32[]{:S(2)}) copy-start(bf16[1024,256]{1,0:T(8,128)(2,1)} %q_ref.3) | copy-start | bytes 1572868
  20.0 18.1 %copy-start.3 = (s32[4]{0:T(128)S(1)}, s32[4]{0:T(128)}, u32[]{:S(2)}) copy-start(s32[4]{0:T(128)} %lengths.3) | copy-start | bytes 52
  20.0 18.1 %copy-start.4 = (s32[8]{0:T(128)S(1)}, s32[8]{0:T(128)}, u32[]{:S(2)}) copy-start(s32[8]{0:T(128)} %counts.3) | copy-start | bytes 100
  20.0 16.9 %collective-permute-start.19 = (bf16[512,128]{1,0:T(8,128)(2,1)S(1)}, bf16[512,128]{1,0:T(8,128)(2,1)S(1)}, u32[]{:S(2)}, u32[]{:S(2)}) collective-permute-start(bf16[512,128]{1,0:T(8,128)(2,1)S(1)} %collective-permute-done.15), channel_id=1, source_target_pairs={{0,4},{1,5},{2,6},{3,7},{4,0},{5,1},{6,2},{7,3},{8,12},{9,13},{10,... | collective-permute-start | bytes 393224 | tf_op jit(solution)/shard_map/ppermute | solution.py:341
  20.3 16.7 %collective-permute-start.21 = (bf16[512,128]{1,0:T(8,128)(2,1)S(1)}, bf16[512,128]{1,0:T(8,128)(2,1)S(1)}, u32[]{:S(2)}, u32[]{:S(2)}) collective-permute-start(bf16[512,128]{1,0:T(8,128)(2,1)S(1)} %collective-permute-done.15), channel_id=1, source_target_pairs={{0,6},{1,7},{2,4},{3,5},{4,2},{5,3},{6,0},{7,1},{8,14},{9,15},{10,... | collective-permute-start | bytes 393224 | tf_op jit(solution)/shard_map/ppermute | solution.py:341
  23.8 13.7 %collective-permute-start.26 = (bf16[512,128]{1,0:T(8,128)(2,1)S(1)}, bf16[512,128]{1,0:T(8,128)(2,1)S(1)}, u32[]{:S(2)}, u32[]{:S(2)}) collective-permute-start(bf16[512,128]{1,0:T(8,128)(2,1)S(1)} %collective-permute-done.25.refs_2_), channel_id=1, source_target_pairs={{0,1},{1,0},{2,3},{3,2},{4,5},{5,4},{6,7},{7,6},{8,9},{9,8},{10,11... | collective-permute-start | bytes 393224 | tf_op jit(solution)/shard_map/ppermute | solution.py:341
  26.8 10.8 %collective-permute-start.28 = (bf16[512,128]{1,0:T(8,128)(2,1)S(1)}, bf16[512,128]{1,0:T(8,128)(2,1)S(1)}, u32[]{:S(2)}, u32[]{:S(2)}) collective-permute-start(bf16[512,128]{1,0:T(8,128)(2,1)S(1)} %collective-permute-done.27.refs_4_), channel_id=1, source_target_pairs={{0,1},{1,0},{2,3},{3,2},{4,5},{5,4},{6,7},{7,6},{8,9},{9,8},{10,11... | collective-permute-start | bytes 393224 | tf_op jit(solution)/shard_map/ppermute | solution.py:341
  27.5 10.6 %collective-permute-start.30 = (bf16[512,128]{1,0:T(8,128)(2,1)S(1)}, bf16[512,128]{1,0:T(8,128)(2,1)S(1)}, u32[]{:S(2)}, u32[]{:S(2)}) collective-permute-start(bf16[512,128]{1,0:T(8,128)(2,1)S(1)} %collective-permute-done.29.refs_6_), channel_id=1, source_target_pairs={{0,1},{1,0},{2,3},{3,2},{4,5},{5,4},{6,7},{7,6},{8,9},{9,8},{10,11... | collective-permute-start | bytes 393224 | tf_op jit(solution)/shard_map/ppermute | solution.py:341
  37.0 10.6 %collective-permute-start.16 = (bf16[512,128]{1,0:T(8,128)(2,1)S(1)}, bf16[512,128]{1,0:T(8,128)(2,1)S(1)}, u32[]{:S(2)}, u32[]{:S(2)}) collective-permute-start(bf16[512,128]{1,0:T(8,128)(2,1)S(1)} %collective-permute-done.15), channel_id=1, source_target_pairs={{0,1},{1,0},{2,3},{3,2},{4,5},{5,4},{6,7},{7,6},{8,9},{9,8},{10,11... | collective-permute-start | bytes 393224 | tf_op jit(solution)/shard_map/ppermute | solution.py:341
  37.1 10.5 %collective-permute-start.18 = (bf16[512,128]{1,0:T(8,128)(2,1)S(1)}, bf16[512,128]{1,0:T(8,128)(2,1)S(1)}, u32[]{:S(2)}, u32[]{:S(2)}) collective-permute-start(bf16[512,128]{1,0:T(8,128)(2,1)S(1)} %collective-permute-done.17), channel_id=1, source_target_pairs={{0,1},{1,0},{2,3},{3,2},{4,5},{5,4},{6,7},{7,6},{8,9},{9,8},{10,11... | collective-permute-start | bytes 393224 | tf_op jit(solution)/shard_map/ppermute | solution.py:341
  37.5 10.0 %collective-permute-start.20 = (bf16[512,128]{1,0:T(8,128)(2,1)S(1)}, bf16[512,128]{1,0:T(8,128)(2,1)S(1)}, u32[]{:S(2)}, u32[]{:S(2)}) collective-permute-start(bf16[512,128]{1,0:T(8,128)(2,1)S(1)} %collective-permute-done.19), channel_id=1, source_target_pairs={{0,1},{1,0},{2,3},{3,2},{4,5},{5,4},{6,7},{7,6},{8,9},{9,8},{10,11... | collective-permute-start | bytes 393224 | tf_op jit(solution)/shard_map/ppermute | solution.py:341
  37.6 9.9 %collective-permute-start.22 = (bf16[512,128]{1,0:T(8,128)(2,1)S(1)}, bf16[512,128]{1,0:T(8,128)(2,1)S(1)}, u32[]{:S(2)}, u32[]{:S(2)}) collective-permute-start(bf16[512,128]{1,0:T(8,128)(2,1)S(1)} %collective-permute-done.21), channel_id=1, source_target_pairs={{0,1},{1,0},{2,3},{3,2},{4,5},{5,4},{6,7},{7,6},{8,9},{9,8},{10,11... | collective-permute-start | bytes 393224 | tf_op jit(solution)/shard_map/ppermute | solution.py:341
  49.5 0.8 %copy-start.5 = (bf16[1024,256]{1,0:T(8,128)(2,1)}, bf16[1024,256]{1,0:T(8,128)(2,1)S(1)}, u32[]{:S(2)}) copy-start(bf16[1024,256]{1,0:T(8,128)(2,1)S(1)} %get-tuple-element.169) | copy-start | bytes 1572868

commit v2 on v1

v2 whole, which is shorter than its diff:
```python
import functools
import math

import jax
import jax.numpy as jnp
from jax import lax
from jax.experimental import pallas as pl
from jax.experimental.pallas import tpu as pltpu
from jax.sharding import PartitionSpec as P

BLOCK = 512
REACH = 7
PAIR = 2
FIELDS = 6
HEADER = 4
NEGATIVE = -1e30
AXES = ("outer", "inner", "head")


def join_kernel(keys, values, joined, semaphores):
    rows = keys.shape[0]
    copies = [
        pltpu.make_async_copy(keys, joined.at[:rows], semaphores.at[0]),
        pltpu.make_async_copy(values, joined.at[rows:], semaphores.at[1]),
    ]
    for copy in copies:
        copy.start()
    for copy in copies:
        copy.wait()


def join(keys, values):
    rows, dim = keys.shape
    return pl.pallas_call(
        join_kernel,
        out_shape=jax.ShapeDtypeStruct((2 * rows, dim), keys.dtype),
        in_specs=[pl.BlockSpec(memory_space=pltpu.MemorySpace.HBM)] * 2,
        out_specs=pl.BlockSpec(memory_space=pltpu.VMEM),
        scratch_shapes=[pltpu.SemaphoreType.DMA((2,))],
        compiler_params=pltpu.CompilerParams(vmem_limit_bytes=4 << 20),
        name="join",
    )(keys, values)


def plan_kernel(cfg, place, lengths, counts, query_source, *refs):
    groups, spread, steps, tile_q, tile_k, further = cfg
    plans = refs[: len(groups)]
    flag, queries, starts, semaphore = refs[len(groups) :]
    copy = pltpu.make_async_copy(query_source, queries, semaphore)
    copy.start()
    context = counts.shape[0]
    documents = lengths.shape[0]
    header = HEADER + documents
    device = place[0]
    head_index = place[1]
    side = head_index // PAIR

    def fill(index, total):
        starts[index] = total
        return total + counts[index] * BLOCK

    starts[context] = lax.fori_loop(0, context, fill, jnp.int32(0))
    own_start = starts[device]
    own_live = counts[device] * BLOCK

    def opening(position):
        def look(index, carry):
            edge, begin = carry
            edge = edge + lengths[index]
            return edge, jnp.where(edge <= position, edge, begin)

        return lax.fori_loop(0, documents, look, (jnp.int32(0), jnp.int32(0)))[1]

    def reaches(level, found):
        before = starts[(level - further + 1) * PAIR]
        return found | (opening(starts[level * PAIR]) < before).astype(jnp.int32)

    flag[0] = lax.fori_loop(further, context // PAIR, reaches, jnp.int32(0))

    for plan, deltas in zip(plans, groups):
        tiles = len(deltas) * PAIR * spread

        def edges(index, edge, plan=plan):
            edge = edge + lengths[index]
            plan[HEADER + index] = edge
            return edge

        lax.fori_loop(0, documents, edges, jnp.int32(0))

        def plan_queries(index, count, plan=plan, deltas=deltas, tiles=tiles):
            row = index * tile_q
            query_start = own_start + row
            query_end = query_start + tile_q - 1
            opened_low = opening(query_start)

            def plan_keys(tile, carry):
                count, opener = carry
                level = device // PAIR - (deltas[0] + tile // (PAIR * spread))
                inner = lax.rem(tile, PAIR * spread)
                member = lax.rem(device, PAIR)
                member = jnp.where(inner // spread == 1, 1 - member, member)
                source = jnp.maximum(level * PAIR + member, 0)
                offset = lax.rem(side + spread - lax.rem(inner, spread), spread) * tile_k
                key_start = starts[source] + offset
                key_end = key_start + tile_k - 1
                active = (
                    (level >= 0)
                    & (row < own_live)
                    & (offset < counts[source] * BLOCK)
                    & (key_start <= query_end)
                    & (key_end >= opened_low)
                )

                @pl.when(active)
                def _():
                    whole = (key_end <= query_start) & (key_start >= opening(key_end))
                    at = header + count * FIELDS
                    plan[at] = index
                    plan[at + 1] = tile
                    plan[at + 2] = whole.astype(jnp.int32)
                    plan[at + 3] = key_start
                    plan[at + 4] = opener
                    plan[at + 5] = 0

                return jnp.where(active, count + 1, count), jnp.where(active, 0, opener)

            after = lax.fori_loop(0, tiles, plan_keys, (count, jnp.int32(1)))[0]

            @pl.when(after > count)
            def _():
                plan[header + (after - 1) * FIELDS + 5] = 1

            return after

        total = lax.fori_loop(0, steps, plan_queries, jnp.int32(0))
        plan[header + total * FIELDS] = 0
        plan[header + total * FIELDS + 1] = 0
        plan[0] = total
        plan[1] = own_start
        plan[2] = own_live
        plan[3] = lax.rem(head_index, PAIR)

    copy.wait()


def make_plans(place, lengths, counts, queries, groups, spread, steps, tile_q, tile_k, further):
    scalar = pl.BlockSpec(memory_space=pltpu.SMEM)
    sizes = [
        HEADER + lengths.shape[0] + FIELDS * (steps * len(deltas) * PAIR * spread + 2)
        for deltas in groups
    ]
    shapes = [jax.ShapeDtypeStruct((size,), jnp.int32) for size in sizes + [1]]
    specs = [scalar] * len(shapes) + [pl.BlockSpec(memory_space=pltpu.VMEM)]
    shapes += [jax.ShapeDtypeStruct(queries.shape, queries.dtype)]
    found = pl.pallas_call(
        functools.partial(plan_kernel, (groups, spread, steps, tile_q, tile_k, further)),
        out_shape=shapes,
        in_specs=[scalar] * 3 + [pl.BlockSpec(memory_space=pltpu.MemorySpace.HBM)],
        out_specs=specs,
        scratch_shapes=[
            pltpu.SMEM((counts.shape[0] + 1,), jnp.int32),
            pltpu.SemaphoreType.DMA,
        ],
        compiler_params=pltpu.CompilerParams(vmem_limit_bytes=4 << 20),
        name="plan",
    )(place, *(in_hbm(array) for array in (lengths, counts, queries)))
    return found[:-2], found[-2], found[-1]


def in_hbm(array):
    return pltpu.with_memory_space_constraint(array, pltpu.MemorySpace.HBM)


def attend_kernel(cfg, plan, q_ref, *refs):
    tiles, heads, tile_q, first, last, documents, count = cfg
    spread = tiles // count
    piece_refs = refs[: PAIR * spread]
    refs = refs[PAIR * spread :]
    if last:
        top_all, acc_all, out_ref = refs[:3]
        refs = refs[3:]
    elif first:
        top_all, acc_all = refs[:2]
        refs = refs[2:]
    else:
        top_all, acc_all = refs[2:4]
        refs = refs[4:]
    k_all, v_all, score_a, score_b, top, acc, opened = refs
    rows = q_ref.shape[0]
    dim = k_all.shape[2]
    tile_k = k_all.shape[1]
    piece = tile_k // PAIR
    scale = math.log2(math.e) / math.sqrt(dim)
    header = HEADER + documents
    total = plan[0]
    own_start = plan[1]
    own_live = plan[2]
    core = plan[3]

    @pl.when(total > 0)
    def _():
        for tile in range(tiles):
            for step in range(PAIR):
                source = piece_refs[(tile % spread) * PAIR + step]
                base = (tile // spread) * 2 * piece
                slot = core if step == 0 else 1 - core
                at = pl.ds(pl.multiple_of(slot * piece, piece), piece)
                k_all[tile, at, :] = source[base : base + piece, :]
                v_all[tile, at, :dim] = source[base + piece : base + 2 * piece, :]
            v_all[tile, :, dim:] = jnp.ones((tile_k, dim), jnp.bfloat16)

    def finish(index, acc_ref):
        at = pl.ds(pl.multiple_of(index * tile_q, tile_q), tile_q)
        for head in range(heads):
            out_ref[at, head * dim : (head + 1) * dim] = (
                acc_ref[head, :, :dim] / acc_ref[head, :, dim:]
            ).astype(jnp.bfloat16)

    def wide(value, times):
        return jnp.concatenate([value] * times, axis=1)

    def score(item, head):
        at = pl.ds(pl.multiple_of(plan[header + item * FIELDS] * tile_q, tile_q), tile_q)
        return lax.dot_general(
            q_ref[at, head * dim : (head + 1) * dim],
            k_all[plan[header + item * FIELDS + 1]],
            (((1,), (1,)), ((), ())),
            preferred_element_type=jnp.float32,
        )

    def handle(item, current, coming):
        base = header + item * FIELDS
        query_index = plan[base]
        whole = plan[base + 2]

        @pl.when(plan[base + 4] == 1)
        def _():
            row = own_start + query_index * tile_q
            position = row + lax.broadcasted_iota(jnp.int32, (tile_q, dim), 0)

            def look(index, unused):
                edge = plan[HEADER + index]
                opened[...] = jnp.where(position >= edge, edge, opened[...])
                return unused

            opened[...] = jnp.zeros((tile_q, dim), jnp.int32)
            lax.fori_loop(0, documents, look, 0)
            if first:
                top[...] = jnp.full(top.shape, NEGATIVE, jnp.float32)
                acc[...] = jnp.zeros(acc.shape, jnp.float32)
            else:
                top[...] = top_all[query_index]
                acc[...] = acc_all[query_index]

        def run(masked):
            v_tile = v_all[plan[base + 1]]
            key_start = plan[base + 3]
            begin = opened[...]
            if masked:
                row = own_start + query_index * tile_q
                position = row + lax.broadcasted_iota(jnp.int32, (tile_q, dim), 0)
                behind = wide((position - begin).astype(jnp.uint32), tile_k // dim)
                key_position = key_start + lax.broadcasted_iota(jnp.int32, (1, tile_k), 1)
            else:
                seen = begin <= key_start
            for head in range(heads):
                coming[head] = score(item + 1, head)
                scores = current[head]
                before = top[head]
                if masked:
                    into = (key_position - wide(begin, tile_k // dim)).astype(jnp.uint32)
                    scores = jnp.where(into <= behind, scores, NEGATIVE)
                    after = jnp.maximum(before, jnp.max(scores, axis=1, keepdims=True))
                    taken = after
                else:
                    after = jnp.maximum(before, jnp.max(scores, axis=1, keepdims=True))
                    after = jnp.where(seen, after, before)
                    taken = jnp.where(seen, after, -NEGATIVE)
                weights = jnp.exp2((scores - wide(taken, tile_k // dim)) * scale)
                factor = jnp.exp2((before - after) * scale)
                top[head] = after
                acc[head] = acc[head] * wide(factor, 2) + jnp.dot(
                    weights.astype(jnp.bfloat16), v_tile, preferred_element_type=jnp.float32
                )

        @pl.when(whole == 1)
        def _():
            run(False)

        @pl.when(whole == 0)
        def _():
            run(True)

        @pl.when(plan[base + 5] == 1)
        def _():
            if last:
                finish(query_index, acc)
            else:
                top_all[query_index] = top[...]
                acc_all[query_index] = acc[...]

    @pl.when(total > 0)
    def _():
        for head in range(heads):
            score_a[head] = score(0, head)

    def two(index, unused):
        handle(2 * index, score_a, score_b)

        @pl.when(2 * index + 1 < total)
        def _():
            handle(2 * index + 1, score_b, score_a)

        return 0

    lax.fori_loop(0, (total + 1) // 2, two, 0)

    if last:

        def rest(index, following):
            row = index * tile_q
            seen = (following < total) & (plan[header + following * FIELDS] == index)

            @pl.when(jnp.logical_not(seen) & (row < own_live))
            def _():
                finish(index, acc_all.at[index])

            @pl.when(row >= own_live)
            def _():
                at = pl.ds(pl.multiple_of(row, tile_q), tile_q)
                out_ref[at, :] = jnp.zeros((tile_q, heads * dim), jnp.bfloat16)

            def skip(item, found):
                return jnp.where(plan[header + item * FIELDS] <= index, found + 1, found)

            return lax.fori_loop(0, total, skip, jnp.int32(0))

        lax.fori_loop(0, rows // tile_q, rest, jnp.int32(0))


def attend(plan, documents, count, queries, pieces, state, last):
    rows, width = queries.shape
    piece_rows, dim = pieces[0].shape
    heads = width // dim
    tile_k = piece_rows // (2 * count) * PAIR
    tiles = len(pieces) // PAIR * count
    tile_q = min(rows, BLOCK)
    steps = rows // tile_q
    first = state is None
    scalar = pl.BlockSpec(memory_space=pltpu.SMEM)
    vector = pl.BlockSpec(memory_space=pltpu.VMEM)
    top = (heads, tile_q, dim)
    acc = (heads, tile_q, 2 * dim)
    scratch = [
        pltpu.VMEM((tiles, tile_k, dim), jnp.bfloat16),
        pltpu.VMEM((tiles, tile_k, 2 * dim), jnp.bfloat16),
        pltpu.VMEM((heads, tile_q, tile_k), jnp.float32),
        pltpu.VMEM((heads, tile_q, tile_k), jnp.float32),
        pltpu.VMEM(top, jnp.float32),
        pltpu.VMEM(acc, jnp.float32),
        pltpu.VMEM((tile_q, dim), jnp.int32),
    ]
    aliases = {}
    if last:
        out_shape = jax.ShapeDtypeStruct((rows, width), jnp.bfloat16)
        out_specs = vector
    else:
        out_shape = (
            jax.ShapeDtypeStruct((steps,) + top, jnp.float32),
            jax.ShapeDtypeStruct((steps,) + acc, jnp.float32),
        )
        out_specs = (vector, vector)
        if not first:
            aliases = {2 + len(pieces): 0, 3 + len(pieces): 1}
    carried = () if first else state
    pairs = steps * tiles * heads
    return pl.pallas_call(
        functools.partial(attend_kernel, (tiles, heads, tile_q, first, last, documents, count)),
        out_shape=out_shape,
        in_specs=[scalar] + [vector] * (1 + len(pieces) + len(carried)),
        out_specs=out_specs,
        scratch_shapes=scratch,
        input_output_aliases=aliases,
        compiler_params=pltpu.CompilerParams(vmem_limit_bytes=24 << 20),
        cost_estimate=pl.CostEstimate(
            flops=pairs * tile_q * tile_k * dim * 4,
            bytes_accessed=pairs * tile_q * dim * 4,
            transcendentals=pairs * tile_q * tile_k,
        ),
    )(plan, queries, *pieces, *carried)


def solution(mesh):
    contexts = mesh.shape["outer"] * mesh.shape["inner"]
    group = mesh.shape["head"]
    levels = contexts // PAIR
    sides = group // PAIR
    farthest = min((REACH + PAIR - 1) // PAIR, levels - 1)
    near_count = min(farthest, 2)

    def moved(value, target):
        pairs = []
        for level in range(levels):
            for member in range(PAIR):
                for side in range(sides):
                    for core in range(PAIR):
                        place = (level, member, side, core)
                        to = target(*place)
                        pairs.append(tuple(
                            ((a * PAIR + b) * sides + c) * PAIR + d for a, b, c, d in (place, to)
                        ))
        return lax.ppermute(value, AXES, pairs)

    def ahead(value, delta):
        return moved(value, lambda l, m, s, c: ((l + delta) % levels, m, s, c))

    def spread(value):
        found = []
        for across in range(PAIR):
            for along in range(sides):
                held = value
                if across or along:
                    held = moved(
                        value, lambda l, m, s, c: (l, (m + across) % PAIR, (s + along) % sides, c)
                    )
                found += [held, moved(held, lambda l, m, s, c: (l, m, s, 1 - c))]
        return found

    def layer(queries, keys, values, lengths, counts):
        device = lax.axis_index(("outer", "inner"))
        place = jnp.stack([device, lax.axis_index("head")]).astype(jnp.int32)

        rows = queries.shape[0]
        tile_q = min(rows, BLOCK)
        groups = [(0,)] + [tuple(range(1, near_count + 1))] * (near_count > 0)
        groups += [(delta,) for delta in range(near_count + 1, farthest + 1)]
        plans, reach, held_queries = make_plans(
            place,
            lengths,
            counts,
            queries,
            groups,
            sides,
            rows // tile_q,
            tile_q,
            keys.shape[0] * PAIR,
            near_count + 1,
        )

        def step(index, pieces, state, last):
            return attend(
                plans[index],
                lengths.shape[0],
                len(groups[index]),
                held_queries,
                pieces,
                state,
                last,
            )

        own = join(in_hbm(keys), in_hbm(values))
        near = [ahead(own, delta) for delta in range(1, near_count + 1)]
        only = near_count == 0
        state = step(0, spread(own), None, only)
        if only:
            return state
        pieces = spread(jnp.concatenate(near, axis=0))
        if farthest == near_count:
            return step(1, pieces, state, True)

        def short(operands):
            _, pieces, state = operands
            return step(1, pieces, state, True)

        def long(operands):
            near, pieces, state = operands
            state = step(1, pieces, state, False)
            for index in range(2, len(groups)):
                near = ahead(near, 1)
                state = step(index, spread(near), state, index == len(groups) - 1)
            return state

        return lax.cond(reach[0] != 0, long, short, (near[-1], pieces, state))

    placed = (
        P(("outer", "inner"), "head"),
        P(AXES, None),
        P(AXES, None),
        P(),
        P(),
    )
    return jax.shard_map(
        layer, mesh=mesh, in_specs=placed, out_specs=P(("outer", "inner"), "head"), check_vma=False
    )
```

time: 50.5 us -> 46 us (0.911)
  local copies, waits for them, and re-layouts: 2.48 us -> 0.82 us
  waiting for transfers between devices: 4.71 us -> 3.09 us
  starting transfers between devices: 22.9 us -> 21.5 us
    unnamed x12 -> x3, local copies, waits for them, and re-layouts: 2.48 us -> 0.8 us
    ppermute x23 -> x16, waiting for transfers between devices: 4.71 us -> 3.09 us  [moved(): return lax.ppermute(value, AXES, pairs)]
    ppermute x23 -> x16, starting transfers between devices: 22.9 us -> 21.5 us  [moved(): return lax.ppermute(value, AXES, pairs)]
    pallas_call x1, Pallas kernels: 0.16 us -> 0.89 us  [join(): pl.pallas_call(join_kernel, out_shape=jax.ShapeDtypeStruct((2 * rows, dim...]
  transfers between devices with their start and end apart: 23 -> 16, of which waited for: 3 -> 4; matrix products, arithmetic and copies ran while one was open for 0% -> 0% of each run, Pallas kernels for 34% -> 20%
where the time goes in v2:
time: 46 us; the launch traced here: 45.8 us
  starting transfers between devices  21.5 us (47%)
  Pallas kernels  19.4 us (42%)
  waiting for transfers between devices  3.09 us (7%)
  local copies, waits for them, and re-layouts  0.82 us (2%)
  between operations  0.75 us (2%)
    ppermute x16, starting transfers between devices, moved(): return lax.ppermute(value, AXES, pairs)  21.5 us
    pallas_call x2, Pallas kernels, attend(): pl.pallas_call(functools.partial(attend_kernel, (tiles, heads, tile_q, fi...  15.4 us
    pallas_call x1, Pallas kernels, make_plans(): pl.pallas_call(functools.partial(plan_kernel, (groups, spread, steps, til...  3.13 us
    ppermute x16, waiting for transfers between devices, moved(): return lax.ppermute(value, AXES, pairs)  3.09 us
  transfers between devices with their start and end apart: 16, of which 4 were waited for; matrix products, arithmetic and copies ran while one was open for 0% of the time, Pallas kernels for 20%

profile of v2, /device:TPU:11, one launch (start us, length us, event | category | flops | bytes accessed | tf_op | source)
XLA Modules:
  0.0 45.8 jit_solution(9426674040785677352)
XLA Ops:
  0.0 0.9 %join.1.refs_0_ = bf16[512,128]{1,0:T(8,128)(2,1)S(1)} custom-call(bf16[256,128]{1,0:T(8,128)(2,1)} %keys.1, bf16[256,128]{1,0:T(8,128)(2,1)} %values.1), custom_call_target="tpu_custom_call" | custom-call | tf_op jit(solution)/shard_map/join/pallas_call | solution.py:34
  0.9 1.3 %collective-permute-start.8 = (bf16[512,128]{1,0:T(8,128)(2,1)S(1)}, bf16[512,128]{1,0:T(8,128)(2,1)S(1)}, u32[]{:S(2)}, u32[]{:S(2)}) collective-permute-start(bf16[512,128]{1,0:T(8,128)(2,1)S(1)} %join.1.refs_0_), channel_id=1, source_target_pairs={{0,8},{1,9},{2,10},{3,11},{4,12},{5,13},{6,14},{7,15},{8,16},{9,17... | collective-permute-start | bytes 393224 | tf_op jit(solution)/shard_map/ppermute | solution.py:412
  2.2 1.1 %collective-permute-start.9 = (bf16[512,128]{1,0:T(8,128)(2,1)S(1)}, bf16[512,128]{1,0:T(8,128)(2,1)S(1)}, u32[]{:S(2)}, u32[]{:S(2)}) collective-permute-start(bf16[512,128]{1,0:T(8,128)(2,1)S(1)} %join.1.refs_0_), channel_id=1, source_target_pairs={{0,16},{1,17},{2,18},{3,19},{4,20},{5,21},{6,22},{7,23},{8,24},{9,... | collective-permute-start | bytes 393224 | tf_op jit(solution)/shard_map/ppermute | solution.py:412
  3.3 1.2 %collective-permute-start.22 = (bf16[512,128]{1,0:T(8,128)(2,1)S(1)}, bf16[512,128]{1,0:T(8,128)(2,1)S(1)}, u32[]{:S(2)}, u32[]{:S(2)}) collective-permute-start(bf16[512,128]{1,0:T(8,128)(2,1)S(1)} %join.1.refs_0_), channel_id=1, source_target_pairs={{0,6},{1,7},{2,4},{3,5},{4,2},{5,3},{6,0},{7,1},{8,14},{9,15},{10,... | collective-permute-start | bytes 393224 | tf_op jit(solution)/shard_map/ppermute | solution.py:412
  4.5 1.2 %collective-permute-start.20 = (bf16[512,128]{1,0:T(8,128)(2,1)S(1)}, bf16[512,128]{1,0:T(8,128)(2,1)S(1)}, u32[]{:S(2)}, u32[]{:S(2)}) collective-permute-start(bf16[512,128]{1,0:T(8,128)(2,1)S(1)} %join.1.refs_0_), channel_id=1, source_target_pairs={{0,4},{1,5},{2,6},{3,7},{4,0},{5,1},{6,2},{7,3},{8,12},{9,13},{10,... | collective-permute-start | bytes 393224 | tf_op jit(solution)/shard_map/ppermute | solution.py:412
  5.8 0.2 collective-permute-start.18
  6.0 0.0 collective-permute-done.8
  6.0 3.9 %collective-permute-start.17 = (bf16[512,128]{1,0:T(8,128)(2,1)S(1)}, bf16[512,128]{1,0:T(8,128)(2,1)S(1)}, u32[]{:S(2)}, u32[]{:S(2)}) collective-permute-start(bf16[512,128]{1,0:T(8,128)(2,1)S(1)} %join.1.refs_0_), channel_id=1, source_target_pairs={{0,1},{1,0},{2,3},{3,2},{4,5},{5,4},{6,7},{7,6},{8,9},{9,8},{10,11... | collective-permute-start | bytes 393224 | tf_op jit(solution)/shard_map/ppermute | solution.py:412
  9.9 0.1 collective-permute-done.9
  10.1 1.3 %collective-permute-start.15 = (bf16[1024,128]{1,0:T(8,128)(2,1)S(1)}, bf16[1024,128]{1,0:T(8,128)(2,1)S(1)}, u32[]{:S(2)}, u32[]{:S(2)}) collective-permute-start(bf16[1024,128]{1,0:T(8,128)(2,1)S(1)} %constant_dynamic-update-slice_fusion), channel_id=1, source_target_pairs={{0,6},{1,7},{2,4},{3,5},{4,2},{5,3},{6,0},{7,1},{8,14},{9,15},{10,... | collective-permute-start | bytes 786440 | tf_op jit(solution)/shard_map/ppermute | solution.py:412
  11.3 0.0 collective-permute-done.22.refs_6_
  11.3 1.2 %collective-permute-start.13 = (bf16[1024,128]{1,0:T(8,128)(2,1)S(1)}, bf16[1024,128]{1,0:T(8,128)(2,1)S(1)}, u32[]{:S(2)}, u32[]{:S(2)}) collective-permute-start(bf16[1024,128]{1,0:T(8,128)(2,1)S(1)} %constant_dynamic-update-slice_fusion), channel_id=1, source_target_pairs={{0,4},{1,5},{2,6},{3,7},{4,0},{5,1},{6,2},{7,3},{8,12},{9,13},{10,... | collective-permute-start | bytes 786440 | tf_op jit(solution)/shard_map/ppermute | solution.py:412
  12.6 0.0 collective-permute-done.20.refs_4_
  12.6 0.2 collective-permute-start.11
  12.8 0.0 collective-permute-done.18.refs_2_
  12.8 2.4 %collective-permute-start.23 = (bf16[512,128]{1,0:T(8,128)(2,1)S(1)}, bf16[512,128]{1,0:T(8,128)(2,1)S(1)}, u32[]{:S(2)}, u32[]{:S(2)}) collective-permute-start(bf16[512,128]{1,0:T(8,128)(2,1)S(1)} %collective-permute-done.22.refs_6_), channel_id=1, source_target_pairs={{0,1},{1,0},{2,3},{3,2},{4,5},{5,4},{6,7},{7,6},{8,9},{9,8},{10,11... | collective-permute-start | bytes 393224 | tf_op jit(solution)/shard_map/ppermute | solution.py:412
  15.2 0.0 collective-permute-done.17.refs_1_
  15.2 0.1 collective-permute-start.21
  15.2 0.9 %collective-permute-done.23.refs_7_ = bf16[512,128]{1,0:T(8,128)(2,1)S(1)} collective-permute-done((bf16[512,128]{1,0:T(8,128)(2,1)S(1)}, bf16[512,128]{1,0:T(8,128)(2,1)S(1)}, u32[]{:S(2)}, u32[]{:S(2)}) %collective-permute-start.23) | collective-permute-done | bytes 131104 | tf_op jit(solution)/shard_map/ppermute | solution.py:412
  16.1 0.4 collective-permute-start.19
  16.5 0.0 collective-permute-done.21.refs_5_
  16.5 0.2 collective-permute-start.10
  16.7 0.7 %collective-permute-done.15 = bf16[1024,128]{1,0:T(8,128)(2,1)S(1)} collective-permute-done((bf16[1024,128]{1,0:T(8,128)(2,1)S(1)}, bf16[1024,128]{1,0:T(8,128)(2,1)S(1)}, u32[]{:S(2)}, u32[]{:S(2)}) %collective-permute-start.15) | collective-permute-done | bytes 262176 | tf_op jit(solution)/shard_map/ppermute | solution.py:412
  17.4 4.4 %collective-permute-start.16 = (bf16[1024,128]{1,0:T(8,128)(2,1)S(1)}, bf16[1024,128]{1,0:T(8,128)(2,1)S(1)}, u32[]{:S(2)}, u32[]{:S(2)}) collective-permute-start(bf16[1024,128]{1,0:T(8,128)(2,1)S(1)} %collective-permute-done.15), channel_id=1, source_target_pairs={{0,1},{1,0},{2,3},{3,2},{4,5},{5,4},{6,7},{7,6},{8,9},{9,8},{10,11... | collective-permute-start | bytes 786440 | tf_op jit(solution)/shard_map/ppermute | solution.py:412
  21.8 1.3 %collective-permute-done.13 = bf16[1024,128]{1,0:T(8,128)(2,1)S(1)} collective-permute-done((bf16[1024,128]{1,0:T(8,128)(2,1)S(1)}, bf16[1024,128]{1,0:T(8,128)(2,1)S(1)}, u32[]{:S(2)}, u32[]{:S(2)}) %collective-permute-start.13) | collective-permute-done | bytes 262176 | tf_op jit(solution)/shard_map/ppermute | solution.py:412
  23.1 2.4 %collective-permute-start.14 = (bf16[1024,128]{1,0:T(8,128)(2,1)S(1)}, bf16[1024,128]{1,0:T(8,128)(2,1)S(1)}, u32[]{:S(2)}, u32[]{:S(2)}) collective-permute-start(bf16[1024,128]{1,0:T(8,128)(2,1)S(1)} %collective-permute-done.13), channel_id=1, source_target_pairs={{0,1},{1,0},{2,3},{3,2},{4,5},{5,4},{6,7},{7,6},{8,9},{9,8},{10,11... | collective-permute-start | bytes 786440 | tf_op jit(solution)/shard_map/ppermute | solution.py:412
  25.5 0.0 collective-permute-done.11
  25.5 0.0 collective-permute-start.12
  25.5 0.1 pad_add_fusion.place
  25.6 3.1 %plan.1 = (s32[68]{0:T(128)S(1)}, s32[116]{0:T(128)S(1)}, s32[68]{0:T(128)S(1)}, s32[1]{0:T(128)}, bf16[1024,256]{1,0:T(8,128)(2,1)S(1)}) custom-call(s32[2]{0:T(128)S(1)} %pad_add_fusion.place, s32[4]{0:T(128)} %lengths.1, s32[8]{0:T(128)} %counts.1, bf16[1024,256]{1,0:T(8,128)(2,1)} %query_source.1), custom_call_target="tpu_custom_call" | custom-call | tf_op jit(solution)/shard_map/plan/pallas_call | solution.py:155
  29.3 0.0 collective-permute-done.19.refs_3_
  29.3 6.2 %shard_map.57 = (f32[2,2,512,128]{3,2,1,0:T(8,128)S(1)}, f32[2,2,512,256]{3,2,1,0:T(8,128)S(1)}) custom-call(s32[68]{0:T(128)S(1)} %get-tuple-element.98.plan, bf16[1024,256]{1,0:T(8,128)(2,1)S(1)} %get-tuple-element.97.q_ref, bf16[512,128]{1,0:T(8,128)(2,1)S(1)} %join.1.refs_0_, bf16[512,128]{1,0:T(8,128)(2,1)S(1)} %collective-permute-done.17.refs_1_, ...), custom_call_target="tpu_custom_call" | custom-call | flops 2147483648 | bytes 4194304 | tf_op jit(solution)/shard_map/pallas_call | solution.py:377
  35.6 0.0 collective-permute-done.10
  35.6 0.0 collective-permute-done.16
  35.6 0.0 collective-permute-done.14
  35.6 0.0 collective-permute-done.12
  35.6 9.4 %conditional.1 = (bf16[1024,256]{1,0:T(8,128)(2,1)S(1)}) conditional(s32[]{:T(128)} %bitcast.2, (s32[116]{0:T(128)S(1)}, bf16[1024,256]{1,0:T(8,128)(2,1)S(1)}, bf16[1024,128]{1,0:T(8,128)(2,1)S(1)}, bf16[1024,128]{1,0:T(8,128)(2,1)S(1)}, bf16[1024,128]{1,0:T(8,128)(2,1)S(1)}, /*index=5*/bf16[1024,128]{1,0:T(8,128)(2,1)S(1)}, ...), branch_computations={%region_0.0_spmd, %region_1.0_spmd} | conditional | flops 6442450944 | bytes 16777544 | solution.py:483
  35.7 9.1 %branch_0_fun.1 = bf16[1024,256]{1,0:T(8,128)(2,1)S(1)} custom-call(s32[116]{0:T(128)S(1)} %get-tuple-element.60.plan, bf16[1024,256]{1,0:T(8,128)(2,1)S(1)} %get-tuple-element.61.q_ref, bf16[1024,128]{1,0:T(8,128)(2,1)S(1)} %get-tuple-element.62.refs_0_, bf16[1024,128]{1,0:T(8,128)(2,1)S(1)} %get-tuple-element.63.refs_1_, ...), custom_call_target="tpu_custom_call" | custom-call | flops 4294967296 | bytes 8388608 | tf_op jit(solution)/shard_map/cond/branch_0_fun/pallas_call | solution.py:377
  45.0 0.0 copy-start
  45.0 0.8 %copy-done = bf16[1024,256]{1,0:T(8,128)(2,1)} copy-done((bf16[1024,256]{1,0:T(8,128)(2,1)}, bf16[1024,256]{1,0:T(8,128)(2,1)S(1)}, u32[]{:S(2)}) %copy-start) | copy-done | bytes 524312
  (2 shorter events, 0.0 us)
Async XLA Ops:
  0.9 5.1 %collective-permute-start.8 = (bf16[512,128]{1,0:T(8,128)(2,1)S(1)}, bf16[512,128]{1,0:T(8,128)(2,1)S(1)}, u32[]{:S(2)}, u32[]{:S(2)}) collective-permute-start(bf16[512,128]{1,0:T(8,128)(2,1)S(1)} %join.1.refs_0_), channel_id=1, source_target_pairs={{0,8},{1,9},{2,10},{3,11},{4,12},{5,13},{6,14},{7,15},{8,16},{9,17... | collective-permute-start | bytes 393224 | tf_op jit(solution)/shard_map/ppermute | solution.py:412
  2.2 7.8 %collective-permute-start.9 = (bf16[512,128]{1,0:T(8,128)(2,1)S(1)}, bf16[512,128]{1,0:T(8,128)(2,1)S(1)}, u32[]{:S(2)}, u32[]{:S(2)}) collective-permute-start(bf16[512,128]{1,0:T(8,128)(2,1)S(1)} %join.1.refs_0_), channel_id=1, source_target_pairs={{0,16},{1,17},{2,18},{3,19},{4,20},{5,21},{6,22},{7,23},{8,24},{9,... | collective-permute-start | bytes 393224 | tf_op jit(solution)/shard_map/ppermute | solution.py:412
  3.3 8.0 %collective-permute-start.22 = (bf16[512,128]{1,0:T(8,128)(2,1)S(1)}, bf16[512,128]{1,0:T(8,128)(2,1)S(1)}, u32[]{:S(2)}, u32[]{:S(2)}) collective-permute-start(bf16[512,128]{1,0:T(8,128)(2,1)S(1)} %join.1.refs_0_), channel_id=1, source_target_pairs={{0,6},{1,7},{2,4},{3,5},{4,2},{5,3},{6,0},{7,1},{8,14},{9,15},{10,... | collective-permute-start | bytes 393224 | tf_op jit(solution)/shard_map/ppermute | solution.py:412
  4.5 8.0 %collective-permute-start.20 = (bf16[512,128]{1,0:T(8,128)(2,1)S(1)}, bf16[512,128]{1,0:T(8,128)(2,1)S(1)}, u32[]{:S(2)}, u32[]{:S(2)}) collective-permute-start(bf16[512,128]{1,0:T(8,128)(2,1)S(1)} %join.1.refs_0_), channel_id=1, source_target_pairs={{0,4},{1,5},{2,6},{3,7},{4,0},{5,1},{6,2},{7,3},{8,12},{9,13},{10,... | collective-permute-start | bytes 393224 | tf_op jit(solution)/shard_map/ppermute | solution.py:412
  5.8 7.0 %collective-permute-start.18 = (bf16[512,128]{1,0:T(8,128)(2,1)S(1)}, bf16[512,128]{1,0:T(8,128)(2,1)S(1)}, u32[]{:S(2)}, u32[]{:S(2)}) collective-permute-start(bf16[512,128]{1,0:T(8,128)(2,1)S(1)} %join.1.refs_0_), channel_id=1, source_target_pairs={{0,2},{1,3},{2,0},{3,1},{4,6},{5,7},{6,4},{7,5},{8,10},{9,11},{10,... | collective-permute-start | bytes 393224 | tf_op jit(solution)/shard_map/ppermute | solution.py:412
  6.0 9.2 %collective-permute-start.17 = (bf16[512,128]{1,0:T(8,128)(2,1)S(1)}, bf16[512,128]{1,0:T(8,128)(2,1)S(1)}, u32[]{:S(2)}, u32[]{:S(2)}) collective-permute-start(bf16[512,128]{1,0:T(8,128)(2,1)S(1)} %join.1.refs_0_), channel_id=1, source_target_pairs={{0,1},{1,0},{2,3},{3,2},{4,5},{5,4},{6,7},{7,6},{8,9},{9,8},{10,11... | collective-permute-start | bytes 393224 | tf_op jit(solution)/shard_map/ppermute | solution.py:412
  10.1 7.3 %collective-permute-start.15 = (bf16[1024,128]{1,0:T(8,128)(2,1)S(1)}, bf16[1024,128]{1,0:T(8,128)(2,1)S(1)}, u32[]{:S(2)}, u32[]{:S(2)}) collective-permute-start(bf16[1024,128]{1,0:T(8,128)(2,1)S(1)} %constant_dynamic-update-slice_fusion), channel_id=1, source_target_pairs={{0,6},{1,7},{2,4},{3,5},{4,2},{5,3},{6,0},{7,1},{8,14},{9,15},{10,... | collective-permute-start | bytes 786440 | tf_op jit(solution)/shard_map/ppermute | solution.py:412
  11.3 11.7 %collective-permute-start.13 = (bf16[1024,128]{1,0:T(8,128)(2,1)S(1)}, bf16[1024,128]{1,0:T(8,128)(2,1)S(1)}, u32[]{:S(2)}, u32[]{:S(2)}) collective-permute-start(bf16[1024,128]{1,0:T(8,128)(2,1)S(1)} %constant_dynamic-update-slice_fusion), channel_id=1, source_target_pairs={{0,4},{1,5},{2,6},{3,7},{4,0},{5,1},{6,2},{7,3},{8,12},{9,13},{10,... | collective-permute-start | bytes 786440 | tf_op jit(solution)/shard_map/ppermute | solution.py:412
  12.6 12.9 %collective-permute-start.11 = (bf16[1024,128]{1,0:T(8,128)(2,1)S(1)}, bf16[1024,128]{1,0:T(8,128)(2,1)S(1)}, u32[]{:S(2)}, u32[]{:S(2)}) collective-permute-start(bf16[1024,128]{1,0:T(8,128)(2,1)S(1)} %constant_dynamic-update-slice_fusion), channel_id=1, source_target_pairs={{0,2},{1,3},{2,0},{3,1},{4,6},{5,7},{6,4},{7,5},{8,10},{9,11},{10,... | collective-permute-start | bytes 786440 | tf_op jit(solution)/shard_map/ppermute | solution.py:412
  12.8 3.4 %collective-permute-start.23 = (bf16[512,128]{1,0:T(8,128)(2,1)S(1)}, bf16[512,128]{1,0:T(8,128)(2,1)S(1)}, u32[]{:S(2)}, u32[]{:S(2)}) collective-permute-start(bf16[512,128]{1,0:T(8,128)(2,1)S(1)} %collective-permute-done.22.refs_6_), channel_id=1, source_target_pairs={{0,1},{1,0},{2,3},{3,2},{4,5},{5,4},{6,7},{7,6},{8,9},{9,8},{10,11... | collective-permute-start | bytes 393224 | tf_op jit(solution)/shard_map/ppermute | solution.py:412
  15.2 1.3 %collective-permute-start.21 = (bf16[512,128]{1,0:T(8,128)(2,1)S(1)}, bf16[512,128]{1,0:T(8,128)(2,1)S(1)}, u32[]{:S(2)}, u32[]{:S(2)}) collective-permute-start(bf16[512,128]{1,0:T(8,128)(2,1)S(1)} %collective-permute-done.20.refs_4_), channel_id=1, source_target_pairs={{0,1},{1,0},{2,3},{3,2},{4,5},{5,4},{6,7},{7,6},{8,9},{9,8},{10,11... | collective-permute-start | bytes 393224 | tf_op jit(solution)/shard_map/ppermute | solution.py:412
  16.1 13.2 %collective-permute-start.19 = (bf16[512,128]{1,0:T(8,128)(2,1)S(1)}, bf16[512,128]{1,0:T(8,128)(2,1)S(1)}, u32[]{:S(2)}, u32[]{:S(2)}) collective-permute-start(bf16[512,128]{1,0:T(8,128)(2,1)S(1)} %collective-permute-done.18.refs_2_), channel_id=1, source_target_pairs={{0,1},{1,0},{2,3},{3,2},{4,5},{5,4},{6,7},{7,6},{8,9},{9,8},{10,11... | collective-permute-start | bytes 393224 | tf_op jit(solution)/shard_map/ppermute | solution.py:412
  16.5 19.1 %collective-permute-start.10 = (bf16[1024,128]{1,0:T(8,128)(2,1)S(1)}, bf16[1024,128]{1,0:T(8,128)(2,1)S(1)}, u32[]{:S(2)}, u32[]{:S(2)}) collective-permute-start(bf16[1024,128]{1,0:T(8,128)(2,1)S(1)} %constant_dynamic-update-slice_fusion), channel_id=1, source_target_pairs={{0,1},{1,0},{2,3},{3,2},{4,5},{5,4},{6,7},{7,6},{8,9},{9,8},{10,11... | collective-permute-start | bytes 786440 | tf_op jit(solution)/shard_map/ppermute | solution.py:412
  17.4 18.2 %collective-permute-start.16 = (bf16[1024,128]{1,0:T(8,128)(2,1)S(1)}, bf16[1024,128]{1,0:T(8,128)(2,1)S(1)}, u32[]{:S(2)}, u32[]{:S(2)}) collective-permute-start(bf16[1024,128]{1,0:T(8,128)(2,1)S(1)} %collective-permute-done.15), channel_id=1, source_target_pairs={{0,1},{1,0},{2,3},{3,2},{4,5},{5,4},{6,7},{7,6},{8,9},{9,8},{10,11... | collective-permute-start | bytes 786440 | tf_op jit(solution)/shard_map/ppermute | solution.py:412
  23.1 12.5 %collective-permute-start.14 = (bf16[1024,128]{1,0:T(8,128)(2,1)S(1)}, bf16[1024,128]{1,0:T(8,128)(2,1)S(1)}, u32[]{:S(2)}, u32[]{:S(2)}) collective-permute-start(bf16[1024,128]{1,0:T(8,128)(2,1)S(1)} %collective-permute-done.13), channel_id=1, source_target_pairs={{0,1},{1,0},{2,3},{3,2},{4,5},{5,4},{6,7},{7,6},{8,9},{9,8},{10,11... | collective-permute-start | bytes 786440 | tf_op jit(solution)/shard_map/ppermute | solution.py:412
  25.5 10.2 %collective-permute-start.12 = (bf16[1024,128]{1,0:T(8,128)(2,1)S(1)}, bf16[1024,128]{1,0:T(8,128)(2,1)S(1)}, u32[]{:S(2)}, u32[]{:S(2)}) collective-permute-start(bf16[1024,128]{1,0:T(8,128)(2,1)S(1)} %collective-permute-done.11), channel_id=1, source_target_pairs={{0,1},{1,0},{2,3},{3,2},{4,5},{5,4},{6,7},{7,6},{8,9},{9,8},{10,11... | collective-permute-start | bytes 786440 | tf_op jit(solution)/shard_map/ppermute | solution.py:412
  45.0 0.8 %copy-start = (bf16[1024,256]{1,0:T(8,128)(2,1)}, bf16[1024,256]{1,0:T(8,128)(2,1)S(1)}, u32[]{:S(2)}) copy-start(bf16[1024,256]{1,0:T(8,128)(2,1)S(1)} %get-tuple-element.153) | copy-start | bytes 1572868
